TPU v7x, 128 devices: a whole 4x4x4 slice. The times are simulated.
128 devices in a mesh: narrow: 4 (over z_lo, core), wide: 32 (over z_hi, x, y).
Axes of the slice: x: 4, y: 4, z: 4 (z_hi: 2, z_lo: 2; z = z_hi * 2 + z_lo), core: 2. Of those that a mesh axis runs over, the one named last changes fastest.
Arguments:
- cand: bfloat16 [2048, 8192], P('wide', 'narrow'), may hold values from -200 to 200
- norm_gain: float32 [8192], P('narrow'), may hold values from 0.5 to 1.5
- gate_weight: bfloat16 [29568, 8192], P('wide', 'narrow'), may hold values from -0.0625 to 0.0625
- up_weight: bfloat16 [29568, 8192], P('wide', 'narrow'), may hold values from -0.0625 to 0.0625
- down_weight: bfloat16 [29568, 8192], P('wide', 'narrow'), may hold values from -0.03125 to 0.03125
- pairs: int32 [8, 2], replicated, may hold values from 0 to 7, as said below
- cand_len: int32 [8], replicated, may hold values from 64 to 256
Outputs:
- ffn_out: bfloat16 [4096, 8192], P('wide', 'narrow')
Inputs may be any that keep to these rules, and one draw needn't show every extreme that they name: `pairs`: the two candidates of a pair differ; every candidate is the first of exactly one pair.
All inputs are finite; a program needn't handle non-finite values.
Results may differ from a plain program's by a relative error of at most 0.0065.
Values may be sent and summed in bfloat16 or wider, within the bound.
A program may use at most 128 MiB of HBM per device.

v0:
```python
import jax
import jax.numpy as jnp
from jax import lax
from jax.sharding import PartitionSpec as P

D = 8192


epsilon = 1e-06


def local(cand, norm_gain, gate_weight, up_weight, down_weight, pairs, cand_len):
    gathered = lax.all_gather(cand, "wide", axis=0, tiled=True)
    values = gathered.astype(jnp.float32)
    squares = lax.psum(jnp.sum(values * values, axis=1), "narrow")
    whole = (values * lax.rsqrt(squares / D + epsilon)[:, None] * norm_gain[None, :]).astype(
        jnp.bfloat16
    )
    cand_tokens = whole.shape[0]
    count = pairs.shape[0]
    length = cand_tokens // count
    positions = jnp.arange(length, dtype=jnp.int32)
    live = (positions[None, :] < cand_len[:, None]).astype(jnp.float32)
    gate = lax.dot_general(
        gate_weight, whole, (((1,), (1,)), ((), ())), preferred_element_type=jnp.float32
    )
    upper = lax.dot_general(
        up_weight, whole, (((1,), (1,)), ((), ())), preferred_element_type=jnp.float32
    )
    gate, upper = (gate, upper)
    gate, upper = (
        lax.psum_scatter(gate, "narrow", scatter_dimension=1, tiled=True),
        lax.psum_scatter(upper, "narrow", scatter_dimension=1, tiled=True),
    )
    hidden = (jax.nn.silu(gate) * upper).astype(jnp.bfloat16)
    terms = lax.dot_general(
        lax.all_gather(hidden, "narrow", axis=1, tiled=True),
        down_weight,
        (((0,), (0,)), ((), ())),
        preferred_element_type=jnp.float32,
    )
    summed = lax.psum_scatter(
        terms * live.reshape(cand_tokens)[:, None], "wide", scatter_dimension=0, tiled=True
    ).astype(jnp.bfloat16)
    spread = lax.all_gather(summed, "wide", axis=0, tiled=True)
    share = 2 * count * length // lax.axis_size("wide")
    token = lax.axis_index("wide") * share + jnp.arange(share, dtype=jnp.int32)
    pair_of = token // (2 * length)
    half = token // length % 2
    place = token % length
    source = pairs[pair_of, half] * length + place
    result = spread[source]
    return result


def solution(mesh):
    return jax.shard_map(
        local,
        mesh=mesh,
        in_specs=(
            P("wide", "narrow"),
            P("narrow"),
            P("wide", "narrow"),
            P("wide", "narrow"),
            P("wide", "narrow"),
            P(),
            P(),
        ),
        out_specs=P("wide", "narrow"),
        check_vma=False,
    )
```

profile of v0, /device:TPU:0, one launch (start us, length us, event | category | flops | bytes accessed | tf_op | source)
XLA Modules:
  0.0 698.4 jit_solution(17817800033256117945)
XLA Ops:
  6.5 0.0 copy-start
  6.5 0.0 all-gather.4.cloned.1.call-start
  6.5 0.7 all-gather.4.cloned.1.call-update
  7.3 0.0 reduce-scatter.4.cloned.1.call-start
  7.3 110.8 %all-gather.4.cloned.1.call-done = bf16[2048,2048]{1,0:T(8,128)(2,1)} async-done(((bf16[64,2048]{1,0:T(8,128)(2,1)}), bf16[2048,2048]{1,0:T(8,128)(2,1)}) %all-gather.4.cloned.1.call-update) | async-done | bytes 8388624 | tf_op jit(solution)/shard_map/all_gather | solution.py:13
  118.1 5.1 fusion
  123.1 6.1 psum.7
  129.2 0.0 copy-done.2
  129.2 13.7 %convolution_bitcast_fusion.1 = f32[924,2048]{1,0:T(8,128)} fusion(bf16[924,2048]{1,0:T(8,128)(2,1)} %param.9, bf16[2048,2048]{1,0:T(8,128)(2,1)} %all-gather.4.cloned.1.call-done, f32[2048]{0:T(1024)S(1)} %copy-done.2, f32[2048]{0:T(1024)S(1)} %add_rsqrt_fusion), kind=kOutput, calls=%fused_computation.9 | convolution fusion | flops 7767851008 | bytes 19759104 | tf_op jit(solution)/shard_map/dot_general | solution.py:24
  143.0 0.0 reduce-scatter.4.cloned.1.call-update
  143.0 0.0 reduce-scatter.6.cloned.1.call-start
  143.0 13.7 %convolution_bitcast_fusion = f32[924,2048]{1,0:T(8,128)} fusion(bf16[924,2048]{1,0:T(8,128)(2,1)} %param.10, bf16[2048,2048]{1,0:T(8,128)(2,1)} %all-gather.4.cloned.1.call-done, f32[2048]{0:T(1024)S(1)} %copy-done.2, f32[2048]{0:T(1024)S(1)} %add_rsqrt_fusion), kind=kOutput, calls=%fused_computation.8 | convolution fusion | flops 7767851008 | bytes 19759104 | tf_op jit(solution)/shard_map/dot_general | solution.py:27
  156.8 0.0 reduce-scatter.6.cloned.1.call-update
  156.8 0.0 all-gather.6.cloned.1.call-start
  156.8 57.4 %reduce-scatter.4.cloned.1.call-done = f32[924,512]{1,0:T(8,128)} async-done(((f32[924,2048]{1,0:T(8,128)}), f32[924,512]{1,0:T(8,128)}) %reduce-scatter.4.cloned.1.call-update) | async-done | bytes 1892368 | tf_op jit(solution)/shard_map/reduce_scatter | solution.py:32
  214.2 76.7 %reduce-scatter.6.cloned.1.call-done = f32[924,512]{1,0:T(8,128)} async-done(((f32[924,2048]{1,0:T(8,128)}), f32[924,512]{1,0:T(8,128)}) %reduce-scatter.6.cloned.1.call-update) | async-done | bytes 1892368 | tf_op jit(solution)/shard_map/reduce_scatter | solution.py:33
  290.9 3.7 multiply_convert_fusion
  294.6 0.0 all-gather.6.cloned.1.call-update
  294.6 0.2 reduce-scatter.8.cloned.1.call-start
  294.8 0.0 copy-done.1
  294.9 0.1 convert_bitcast_fusion
  294.9 43.7 %all-gather.6.cloned.1.call-done = bf16[924,2048]{1,0:T(8,128)(2,1)} async-done(((bf16[924,512]{1,0:T(8,128)(2,1)}), bf16[924,2048]{1,0:T(8,128)(2,1)}) %all-gather.6.cloned.1.call-update) | async-done | bytes 3784720 | tf_op jit(solution)/shard_map/all_gather | solution.py:37
  338.6 15.1 %convolution_multiply_fusion = f32[2048,2048]{1,0:T(8,128)} fusion(bf16[924,2048]{1,0:T(8,128)(2,1)} %all-gather.6.cloned.1.call-done, bf16[924,2048]{1,0:T(8,128)(2,1)} %param.11, f32[2048]{0:T(1024)S(1)} %bitcast.19), kind=kOutput, calls=%fused_computation.7 | convolution fusion | flops 7755268096 | bytes 24354816 | tf_op jit(solution)/shard_map/dot_general | solution.py:36
  353.7 0.0 reduce-scatter.8.cloned.1.call-update
  353.8 0.0 all-gather.8.cloned.1.call-start
  353.8 226.0 %reduce-scatter.8.cloned.1.call-done = f32[64,2048]{1,0:T(8,128)} async-done(((f32[2048,2048]{1,0:T(8,128)}), f32[64,2048]{1,0:T(8,128)}) %reduce-scatter.8.cloned.1.call-update) | async-done | bytes 524304 | tf_op jit(solution)/shard_map/reduce_scatter | solution.py:42
  579.8 1.8 convert_element_type.27
  581.6 0.0 all-gather.8.cloned.1.call-update
  581.6 0.0 copy-done
  581.7 1.5 gather_fusion
  583.2 101.6 %all-gather.8.cloned.1.call-done = bf16[2048,2048]{1,0:T(8,128)(2,1)} async-done(((bf16[64,2048]{1,0:T(8,128)(2,1)}), bf16[2048,2048]{1,0:T(8,128)(2,1)}) %all-gather.8.cloned.1.call-update) | async-done | bytes 8388624 | tf_op jit(solution)/shard_map/all_gather | solution.py:45
  684.8 6.7 gather_fusion.1
  (7 shorter events, 0.1 us)
Async XLA Ops:
  6.5 575.1 %copy-start = (s32[8,2]{0,1:T(2,128)S(1)}, s32[8,2]{0,1:T(2,128)}, u32[]{:S(2)}) copy-start(s32[8,2]{0,1:T(2,128)} %param.12) | copy-start | bytes 196
  6.5 122.7 %copy-start.2 = (f32[2048]{0:T(1024)S(1)}, f32[2048]{0:T(1024)}, u32[]{:S(2)}) copy-start(f32[2048]{0:T(1024)} %param.8) | copy-start | bytes 24580
  6.5 111.5 %all-gather.4.cloned.1.call-start = ((), (), s32[]{:S(2)}) async-start(), calls=%async_computation.3 | async-start | bytes 8650752 | tf_op jit(solution)/shard_map/all_gather | solution.py:13
  7.3 207.0 %reduce-scatter.4.cloned.1.call-start = ((), (), s32[]{:S(2)}) async-start(), calls=%async_computation.4 | async-start | bytes 9502720 | tf_op jit(solution)/shard_map/reduce_scatter | solution.py:32
  143.0 147.9 %reduce-scatter.6.cloned.1.call-start = ((), (), s32[]{:S(2)}) async-start(), calls=%async_computation.5 | async-start | bytes 9502720 | tf_op jit(solution)/shard_map/reduce_scatter | solution.py:33
  156.8 138.1 %copy-start.1 = (s32[8]{0:T(128)S(1)}, s32[8]{0:T(128)}, u32[]{:S(2)}) copy-start(s32[8]{0:T(128)} %param.13) | copy-start | bytes 100
  156.8 181.8 %all-gather.6.cloned.1.call-start = ((), (), s32[]{:S(2)}) async-start(), calls=%async_computation.6 | async-start | bytes 4751360 | tf_op jit(solution)/shard_map/all_gather | solution.py:37
  294.6 285.2 %reduce-scatter.8.cloned.1.call-start = ((), (), s32[]{:S(2)}) async-start(), calls=%async_computation.7 | async-start | bytes 17301504 | tf_op jit(solution)/shard_map/reduce_scatter | solution.py:42
  353.8 331.1 %all-gather.8.cloned.1.call-start = ((), (), s32[]{:S(2)}) async-start(), calls=%async_computation.8 | async-start | bytes 8650752 | tf_op jit(solution)/shard_map/all_gather | solution.py:45
Sparse Core Ops, SparseCore 0:
  10.5 107.5 all-gather.3
  143.1 71.0 reduce-scatter.3
  216.7 74.2 reduce-scatter.5
  294.7 43.8 all-gather.5
  353.9 225.8 reduce-scatter.7
  582.8 102.0 all-gather.7
where the time goes:
time: 699 us; the launch traced here: 698 us
  waiting for transfers between devices  617 us (88%)
  matrix products  42.6 us (6%)
  between operations  13.5 us (2%)
  other arithmetic  10.6 us (2%)
  local copies, waits for them, and re-layouts  8.22 us (1%)
    reduce_scatter x1, waiting for transfers between devices, local(): lax.psum_scatter(terms * live.reshape(cand_tokens)[:, None], 'wide', scat...  226 us
    all_gather x1, waiting for transfers between devices, local(): gathered = lax.all_gather(cand, 'wide', axis=0, tiled=True)  111 us
    all_gather x1, waiting for transfers between devices, local(): spread = lax.all_gather(summed, 'wide', axis=0, tiled=True)  102 us
    reduce_scatter x1, waiting for transfers between devices, local(): lax.psum_scatter(upper, 'narrow', scatter_dimension=1, tiled=True)  76.7 us
    reduce_scatter x1, waiting for transfers between devices, local(): lax.psum_scatter(gate, 'narrow', scatter_dimension=1, tiled=True)  57.4 us
    all_gather x1, waiting for transfers between devices, local(): lax.all_gather(hidden, 'narrow', axis=1, tiled=True)  43.7 us
    dot_general x1, matrix products, local(): lax.dot_general(lax.all_gather(hidden, 'narrow', axis=1, tiled=True), dow...  15.1 us
  transfers between devices with their start and end apart: 6, of which 6 were waited for; matrix products, arithmetic and copies ran while one was open for 2% of the time, Pallas kernels for 0%

commit v1 on v0

v1 whole, which is shorter than its diff:
```python
import functools

import jax
import jax.numpy as jnp
from jax import lax
from jax.experimental import pallas as pl
from jax.experimental.pallas import tpu as pltpu
from jax.sharding import PartitionSpec as P

MESH = pl.DeviceIdType.MESH
F32 = jnp.float32
BF16 = jnp.bfloat16


class Net:
    def __init__(self, send_sem, recv_sem):
        self.send_sem, self.recv_sem = send_sem, recv_sem
        self.index, self.sent = {}, []

    def slot(self, key):
        return self.index.setdefault(key, len(self.index))

    def send(self, key, src, dst, device):
        i = self.slot(key)
        copy = pltpu.make_async_remote_copy(
            src_ref=src, dst_ref=dst, send_sem=self.send_sem.at[i], recv_sem=self.recv_sem.at[i],
            device_id=device, device_id_type=MESH,
        )
        copy.start()
        self.sent.append(copy)
        return copy

    def recv(self, key, dst, device):
        i = self.slot(key)
        pltpu.make_async_remote_copy(
            src_ref=dst, dst_ref=dst, send_sem=self.send_sem.at[i], recv_sem=self.recv_sem.at[i],
            device_id=device, device_id_type=MESH,
        ).wait_recv()

    def finish(self):
        for copy in self.sent:
            copy.wait_send()


def position():
    w = lax.axis_index("wide")
    return w // 16, (w // 4) % 4, w % 4


def wide_of(c, z, p, q):
    x, y = (p, q) if c == 0 else (q, p)
    return {"wide": z * 16 + ((x + 8) % 4) * 4 + (y + 8) % 4}


def coords(c, x, y):
    return (x, y) if c == 0 else (y, x)


def mod4(a):
    return (a + 8) % 4


def barrier_wide():
    z, x, y = position()
    sem = pltpu.get_barrier_semaphore()
    for dev in (
        wide_of(0, z, x + 1, y), wide_of(0, z, x - 1, y),
        wide_of(0, z, x, y + 1), wide_of(0, z, x, y - 1), wide_of(0, 1 - z, x, y),
    ):
        pl.semaphore_signal(sem, inc=1, device_id=dev, device_id_type=MESH)
    pl.semaphore_wait(sem, 5)


def all_gather_wide(net, tag, reg, reg2):
    z, x, y = position()

    def r1(c, zz, p, q):
        a, b = coords(c, mod4(p), mod4(q))
        return reg(c, zz, a, b)

    def r2(c, p, q):
        a, b = coords(c, mod4(p), mod4(q))
        return reg2(c, a, b)

    def send(key, region, c, dz, p, q):
        net.send((tag,) + key, region, region, wide_of(c, dz, p, q))

    def recv(key, region, c):
        net.recv((tag,) + key, region, wide_of(c, z, x, y))

    pq = [coords(0, x, y), coords(1, x, y)]
    half = {1: 0, -1: 1}
    for c in (0, 1):
        p, q = pq[c]
        send(("z", c), r1(c, z, p, q), c, 1 - z, p, q)
    for s in (1, -1):
        for c in (0, 1):
            p, q = pq[c]
            send(("p1", c, s, 0), r1(c, z, p, q), c, z, p + s, q)
    for c in (0, 1):
        p, q = pq[c]
        recv(("z", c), r1(c, 1 - z, p, q), c)
        for s in (1, -1):
            send(("p1", c, s, 1), r1(c, 1 - z, p, q), c, z, p + s, q)
    for c in (0, 1):
        p, q = pq[c]
        for s in (1, -1):
            send(("q1", c, s, 0), r2(c, p, q), c, z, p, q + s)
    for s in (1, -1):
        for c in (0, 1):
            p, q = pq[c]
            recv(("p1", c, s, 0), r1(c, z, p - s, q), c)
            recv(("p1", c, s, 1), r1(c, 1 - z, p - s, q), c)
            send(("p2", c, s), r1(c, half[s], p - s, q), c, z, p + s, q)
    for s in (1, -1):
        for c in (0, 1):
            p, q = pq[c]
            for t in (1, -1):
                send(("q1", c, t, -s), r2(c, p - s, q), c, z, p, q + t)
    for c in (0, 1):
        p, q = pq[c]
        for s in (1, -1):
            recv(("p2", c, s), r1(c, half[s], p - 2 * s, q), c)
        for t in (1, -1):
            send(("q1", c, t, 2), r2(c, p + 2, q), c, z, p, q + t)
    for rel in (0, -1, 1, 2):
        for s in (1, -1):
            for c in (0, 1):
                p, q = pq[c]
                recv(("q1", c, s, rel), r2(c, p + rel, q - s), c)
                send(("q2", c, s, rel), r1(c, half[s], p + rel, q - s), c, z, p, q + s)
    for rel in (0, -1, 1, 2):
        for s in (1, -1):
            for c in (0, 1):
                p, q = pq[c]
                recv(("q2", c, s, rel), r1(c, half[s], p + rel, q - 2 * s), c)


AG_MESSAGES = 2 * (1 + 4 + 2 + 8 + 8)


def gather_kernel(own_ref, out_ref, copy_sem, send_sem, recv_sem):
    z, x, y = position()
    copy = pltpu.make_async_copy(own_ref, out_ref.at[z, x, y], copy_sem)
    copy.start()
    barrier_wide()
    copy.wait()
    net = Net(send_sem, recv_sem)
    half = own_ref.shape[1] // 2

    def reg(c, zz, a, b):
        return out_ref.at[zz, a, b, :, pl.ds(c * half, half)]

    def reg2(c, a, b):
        return out_ref.at[:, a, b, :, pl.ds(c * half, half)]

    all_gather_wide(net, "g", reg, reg2)
    net.finish()


def gather_wide(own, collective_id=0):
    rows, cols = own.shape
    out = pl.pallas_call(
        gather_kernel,
        out_shape=jax.ShapeDtypeStruct((2, 4, 4, rows, cols), own.dtype),
        in_specs=[pl.BlockSpec(memory_space=pltpu.VMEM)],
        out_specs=pl.BlockSpec(memory_space=pl.ANY),
        scratch_shapes=[
            pltpu.SemaphoreType.DMA,
            pltpu.SemaphoreType.DMA((AG_MESSAGES,)),
            pltpu.SemaphoreType.DMA((AG_MESSAGES,)),
        ],
        compiler_params=pltpu.CompilerParams(collective_id=collective_id, has_side_effects=True),
        name="gather_tokens",
    )(own)
    return out.reshape(32 * rows, cols)


def add_rows(dst, srcs, rows, step=16):
    def body(i, carry):
        at = pl.ds(pl.multiple_of(i * step, step), step)
        total = srcs[0][at, :].astype(F32)
        for src in srcs[1:]:
            total = total + src[at, :].astype(F32)
        dst[at, :] = total.astype(dst.dtype)
        return carry

    lax.fori_loop(0, rows // step, body, 0)


def reduce_ring(net, tag, c, axis, unit, rows, r1, r2, sb):
    z, x, y = position()
    p, q = coords(c, x, y)
    me = p if axis == "p" else q

    def dev(s):
        return wide_of(c, z, p + s, q) if axis == "p" else wide_of(c, z, p, q + s)

    hr = rows // 2
    half = {1: 0, -1: 1}

    def part(ref, h):
        return ref.at[pl.ds(h * hr, hr), :]

    def first():
        for s in (1, -1):
            net.send((tag, "r1", c, s), part(unit(mod4(me + 2)), half[s]), r1.at[half[s]], dev(s))

    def direct():
        for s in (1, -1):
            o = 1 - half[s]
            net.send((tag, "r2d", c, s), part(unit(mod4(me + s)), o), part(r2.at[half[s]], o), dev(s))

    def middle():
        for s in (1, -1):
            h = half[s]
            net.recv((tag, "r1", c, s), r1.at[h], dev(s))
            add_rows(sb.at[h], [part(unit(mod4(me + s)), h), r1.at[h]], hr)
            net.send((tag, "r2s", c, s), sb.at[h], part(r2.at[h], h), dev(s))

    def end(dst):
        for s in (1, -1):
            h = half[s]
            net.recv((tag, "r2d", c, s), part(r2.at[h], 1 - h), dev(s))
            net.recv((tag, "r2s", c, s), part(r2.at[h], h), dev(s))
        add_rows(dst, [unit(mod4(me)), r2.at[0], r2.at[1]], rows)

    return first, direct, middle, end


def reduce_scatter_wide(net, part_ref, bufs, dst, tiles):
    z, x, y = position()
    T = part_ref.shape[0]
    C = part_ref.shape[1] // 2
    K = C // 4
    Q = [bufs["q0"], bufs["q1"]]

    def big(c):
        if c == 0:
            return lambda j: part_ref.at[pl.ds(pl.multiple_of(j * (T // 4), 16), T // 4), pl.ds(0, C)]
        return lambda j: part_ref.at[:, pl.ds(pl.multiple_of(C + j * K, 128), K)]

    def small(c):
        if c == 0:
            return lambda j: Q[0].at[:, pl.ds(pl.multiple_of(j * K, 128), K)]
        return lambda j: Q[1].at[pl.ds(pl.multiple_of(j * (T // 4), 16), T // 4), :]

    rows = [T // 4, T]
    one = [reduce_ring(net, "a", c, "q", big(c), rows[c], bufs[f"r1{c}"], bufs[f"r2{c}"], bufs[f"sb{c}"]) for c in (0, 1)]
    two = [reduce_ring(net, "b", c, "p", small(c), T // 4, bufs[f"s1{c}"], bufs[f"s2{c}"], bufs[f"tb{c}"]) for c in (0, 1)]
    tiles(2)
    for c in (0, 1):
        one[c][0]()
    tiles(1)
    tiles(-1)
    for c in (0, 1):
        one[c][1]()
    for c in (0, 1):
        one[c][2]()
    tiles(0)
    for c in (0, 1):
        one[c][3](Q[c])
        two[c][0]()
        two[c][1]()
    for c in (0, 1):
        two[c][2]()
    H = T // 8
    for c in (0, 1):
        w = bufs[f"w{c}"]
        two[c][3](w)
        p, q = coords(c, x, y)
        net.send(("c", c), w.at[pl.ds(pl.multiple_of((1 - z) * H, 16), H), :], bufs[f"v{c}"], wide_of(c, 1 - z, p, q))
    for c in (0, 1):
        p, q = coords(c, x, y)
        net.recv(("c", c), bufs[f"v{c}"], wide_of(c, 1 - z, p, q))
        w = bufs[f"w{c}"]
        add_rows(dst(c), [w.at[pl.ds(pl.multiple_of(z * H, 16), H), :], bufs[f"v{c}"]], H)


RS_MESSAGES = 2 * (6 + 6 + 1)


def reduce_bufs(T, C):
    K = C // 4
    shapes = {}
    for c, (rows, cols) in enumerate(((T // 4, C), (T, K))):
        shapes[f"q{c}"] = (rows, cols)
        shapes[f"r1{c}"] = (2, rows // 2, cols)
        shapes[f"r2{c}"] = (2, rows, cols)
        shapes[f"sb{c}"] = (2, rows // 2, cols)
        shapes[f"s1{c}"] = (2, T // 8, K)
        shapes[f"s2{c}"] = (2, T // 4, K)
        shapes[f"tb{c}"] = (2, T // 8, K)
        shapes[f"w{c}"] = (T // 4, K)
        shapes[f"v{c}"] = (T // 8, K)
    return shapes


def barrier_narrow():
    n = lax.axis_index("narrow")
    sem = pltpu.get_barrier_semaphore()
    for dev in (n + 1 - 2 * (n % 2), (n + 2) % 4):
        pl.semaphore_signal(sem, inc=1, device_id={"narrow": dev}, device_id_type=MESH)
    pl.semaphore_wait(sem, 2)


TILES = 8
PAIRS_OF = 5


def hidden_kernel(
    x_ref, gate_ref, up_ref, tail_ref, hid_ref,
    w_ref, own_ref, sa, ra, sz, rz, sb, rb,
    w_sem, a_send, a_recv, z_send, z_recv, b_send, b_recv, hc_send, hc_recv, hz_send, hz_recv, hf_send, hf_recv,
):
    n = lax.axis_index("narrow")
    zl, co = n // 2, n % 2
    core, far = zl * 2 + 1 - co, (1 - zl) * 2 + co
    T = x_ref.shape[0]
    M = T // 4
    loads = []
    for k in range(3):
        loads.append((gate_ref.at[pl.ds(k * 256, 256), :], w_ref.at[pl.ds(k * 512, 256), :]))
        loads.append((up_ref.at[pl.ds(k * 256, 256), :], w_ref.at[pl.ds(k * 512 + 256, 256), :]))
    loads.append((gate_ref.at[pl.ds(768, 128), :], w_ref.at[pl.ds(1536, 128), :]))
    loads.append((up_ref.at[pl.ds(768, 128), :], w_ref.at[pl.ds(1664, 128), :]))
    loads.append((tail_ref, w_ref.at[pl.ds(1792, 128), :]))
    loads = [pltpu.make_async_copy(s, d, w_sem.at[i]) for i, (s, d) in enumerate(loads)]
    for copy in loads:
        copy.start()
    barrier_narrow()
    for copy in loads:
        copy.wait()

    def link(src, dst, send, recv, device):
        return pltpu.make_async_remote_copy(
            src_ref=src, dst_ref=dst, send_sem=send, recv_sem=recv, device_id={"narrow": device}, device_id_type=MESH
        )

    def product(block, at, width):
        rows = x_ref[pl.ds(pl.multiple_of(block * M, 32), M), :]
        return lax.dot_general(
            rows, w_ref[pl.ds(at, width), :], (((1,), (1,)), ((), ())), preferred_element_type=F32
        )

    def tiles(block, use):
        def body(j, carry):
            at = pl.multiple_of(j * 256, 256)
            use(j, at, 256, product(block, at, 256))
            return carry

        lax.fori_loop(0, 7, body, 0)
        use(7, 1792, 128, product(block, 1792, 128))

    def cut(ref, at, width):
        return ref.at[:, pl.ds(at, width)]

    def to_core(s, r, send, recv):
        def use(j, at, width, value):
            cut(s, at, width)[...] = value.astype(BF16)
            link(cut(s, at, width), cut(r, at, width), send.at[j], recv.at[j], core).start()

        return use

    def to_far(j, at, width, value):
        link(cut(ra, at, width), cut(ra, at, width), a_send.at[j], a_recv.at[j], core).wait_recv()
        cut(sz, at, width)[...] = (value + cut(ra, at, width)[...].astype(F32)).astype(BF16)
        link(cut(sz, at, width), cut(rz, at, width), z_send.at[j], z_recv.at[j], far).start()

    def keep(j, at, width, value):
        link(cut(rb, at, width), cut(rb, at, width), b_send.at[j], b_recv.at[j], core).wait_recv()
        cut(own_ref, at, width)[...] = value + cut(rb, at, width)[...].astype(F32)

    tiles((1 - zl) * 2 + 1 - co, to_core(sa, ra, a_send, a_recv))
    tiles((1 - zl) * 2 + co, to_far)
    tiles(zl * 2 + 1 - co, to_core(sb, rb, b_send, b_recv))
    tiles(n, keep)

    def await_far(j, at, width):
        link(cut(rz, at, width), cut(rz, at, width), z_send.at[j], z_recv.at[j], far).wait_recv()

    def total(at, width, r):
        return own_ref[r, pl.ds(at, width)] + rz[r, pl.ds(at, width)].astype(F32)

    def gated(g, u):
        return (g / (1.0 + jnp.exp(-g)) * u).astype(BF16)

    def hid(block, at, width):
        return hid_ref.at[pl.ds(pl.multiple_of(block * M, 32), M), pl.ds(at, width)]

    def rows_of(block, i):
        return pl.ds(pl.multiple_of(block * M + i * 32, 32), 32)

    def over_rows(fill):
        def body(i, carry):
            fill(i, pl.ds(pl.multiple_of(i * 32, 32), 32))
            return carry

        lax.fori_loop(0, M // 32, body, 0)

    def spread(k, at, width):
        mine = hid(n, at, width)
        link(mine, mine, hz_send.at[k], hz_recv.at[k], far).start()
        link(mine, mine, hc_send.at[k], hc_recv.at[k], core).start()

    def pair(k, carry):
        g, u, h = (pl.multiple_of(v, 256) for v in (k * 512, k * 512 + 256, k * 256))
        await_far(2 * k, g, 256)
        await_far(2 * k + 1, u, 256)

        def fill(i, r):
            hid_ref[rows_of(n, i), pl.ds(h, 256)] = gated(total(g, 256, r), total(u, 256, r))

        over_rows(fill)
        spread(k, h, 256)
        return carry

    lax.fori_loop(0, 3, pair, 0)
    await_far(6, 1536, 256)

    def fill3(i, r):
        hid_ref[rows_of(n, i), pl.ds(768, 128)] = gated(total(1536, 128, r), total(1664, 128, r))

    over_rows(fill3)
    spread(3, 768, 128)
    await_far(7, 1792, 128)

    def fill4(i, r):
        g = total(1792, 128, r)
        hid_ref[rows_of(n, i), pl.ds(896, 128)] = gated(g, pltpu.roll(g, 64, 1))

    over_rows(fill4)
    spread(4, 896, 128)

    cols = [(k, k * 256, 256) for k in range(3)] + [(3, 768, 128), (4, 896, 128)]
    for k, at, width in cols:
        theirs = hid(far, at, width)
        link(theirs, theirs, hz_send.at[k], hz_recv.at[k], far).wait_recv()
        link(theirs, theirs, hf_send.at[k], hf_recv.at[k], core).start()
    for k, at, width in cols:
        theirs = hid(core, at, width)
        link(theirs, theirs, hc_send.at[k], hc_recv.at[k], core).wait_recv()
    for k, at, width in cols:
        theirs = hid((1 - zl) * 2 + 1 - co, at, width)
        link(theirs, theirs, hf_send.at[k], hf_recv.at[k], core).wait_recv()
    for j in range(TILES):
        at, width = j * 256, (256 if j < 7 else 128)
        for s, send, recv in ((sa, a_send, a_recv), (sz, z_send, z_recv), (sb, b_send, b_recv)):
            link(cut(s, at, width), cut(s, at, width), send.at[j], recv.at[j], core).wait_send()
    for k, at, width in cols:
        mine = hid(n, at, width)
        link(mine, mine, hz_send.at[k], hz_recv.at[k], far).wait_send()
        link(mine, mine, hc_send.at[k], hc_recv.at[k], core).wait_send()
        theirs = hid(far, at, width)
        link(theirs, theirs, hf_send.at[k], hf_recv.at[k], core).wait_send()


def hidden_units(x, gate_weight, up_weight, tail, collective_id):
    T, D = x.shape
    M = T // 4
    N = 1920
    DMA = pltpu.SemaphoreType.DMA
    return pl.pallas_call(
        hidden_kernel,
        out_shape=jax.ShapeDtypeStruct((T, 1024), BF16),
        in_specs=[
            pl.BlockSpec(memory_space=pltpu.VMEM),
            pl.BlockSpec(memory_space=pl.ANY),
            pl.BlockSpec(memory_space=pl.ANY),
            pl.BlockSpec(memory_space=pl.ANY),
        ],
        out_specs=pl.BlockSpec(memory_space=pltpu.VMEM),
        scratch_shapes=[pltpu.VMEM((N, D), BF16), pltpu.VMEM((M, N), F32)]
        + [pltpu.VMEM((M, N), BF16)] * 6
        + [DMA((9,))] + [DMA((TILES,))] * 6 + [DMA((PAIRS_OF,))] * 6,
        compiler_params=pltpu.CompilerParams(
            collective_id=collective_id, has_side_effects=True, vmem_limit_bytes=62 * 2**20
        ),
        name="hidden_units",
    )(x, gate_weight, up_weight, tail)


def output_kernel(names, hid_ref, down_ref, tail_ref, out_ref, d_ref, part_ref, d_sem, copy_sem, send_sem, recv_sem, *scratch):
    bufs = dict(zip(names, scratch))
    z, x, y = position()
    T, cols = part_ref.shape
    C = cols // 2
    K = C // 4
    loads = [
        pltpu.make_async_copy(down_ref.at[pl.ds(0, 896), :], d_ref.at[pl.ds(0, 896), :], d_sem.at[0]),
        pltpu.make_async_copy(tail_ref, d_ref.at[pl.ds(896, 128), :], d_sem.at[1]),
    ]
    for copy in loads:
        copy.start()
    barrier_wide()
    for copy in loads:
        copy.wait()
    net = Net(send_sem, recv_sem)

    def tile(r, k):
        rows = pl.ds(pl.multiple_of(r * (T // 4), 32), T // 4)
        at = pl.ds(pl.multiple_of(k * 256, 256), 256)
        part_ref[rows, at] = jnp.dot(hid_ref[rows, :], d_ref[:, at], preferred_element_type=F32).astype(BF16)

    def tiles(dq):
        def body(i, carry):
            tile(mod4(y + dq), i)
            tile(i, 4 + mod4(x + dq))
            return carry

        lax.fori_loop(0, 4, body, 0)

    reduce_scatter_wide(net, part_ref, bufs, lambda c: bufs["res"].at[c], tiles)

    def reg(c, zz, a, b):
        return out_ref.at[
            pl.ds(pl.multiple_of(b * (T // 4) + zz * (T // 8), 16), T // 8),
            pl.ds(pl.multiple_of(c * C + a * K, 128), K),
        ]

    def reg2(c, a, b):
        return out_ref.at[
            pl.ds(pl.multiple_of(b * (T // 4), 16), T // 4), pl.ds(pl.multiple_of(c * C + a * K, 128), K)
        ]

    copies = []
    for c in (0, 1):
        copy = pltpu.make_async_copy(bufs["res"].at[c], reg(c, z, x, y), copy_sem.at[c])
        copy.start()
        copies.append(copy)
    for copy in copies:
        copy.wait()
    all_gather_wide(net, "g", reg, reg2)
    net.finish()


def outputs(hid, down_weight, tail, collective_id):
    T = hid.shape[0]
    cols = down_weight.shape[1]
    C = cols // 2
    shapes = reduce_bufs(T, C)
    shapes["res"] = (2, T // 8, C // 4)
    names = tuple(shapes)
    n = AG_MESSAGES + RS_MESSAGES
    return pl.pallas_call(
        functools.partial(output_kernel, names),
        out_shape=jax.ShapeDtypeStruct((T, cols), BF16),
        in_specs=[
            pl.BlockSpec(memory_space=pltpu.VMEM),
            pl.BlockSpec(memory_space=pl.ANY),
            pl.BlockSpec(memory_space=pl.ANY),
        ],
        out_specs=pl.BlockSpec(memory_space=pl.ANY),
        scratch_shapes=[
            pltpu.VMEM((1024, cols), BF16),
            pltpu.VMEM((T, cols), BF16),
            pltpu.SemaphoreType.DMA((2,)),
            pltpu.SemaphoreType.DMA((2,)),
            pltpu.SemaphoreType.DMA((n,)),
            pltpu.SemaphoreType.DMA((n,)),
        ] + [pltpu.VMEM(shapes[k], BF16) for k in names],
        compiler_params=pltpu.CompilerParams(
            collective_id=collective_id, has_side_effects=True, vmem_limit_bytes=62 * 2**20
        ),
        name="reduce_outputs",
    )(hid, down_weight, tail)


STEP = 16


def blocks_of(length):
    return (length + STEP - 1) // STEP


def compact_kernel(len_ref, all_ref, out_ref, sem):
    T = out_ref.shape[0]
    count = len_ref.shape[0]
    length = all_ref.shape[0] // count

    def copy(src, dst):
        pltpu.make_async_copy(
            all_ref.at[pl.ds(pl.multiple_of(src, STEP), STEP), :],
            out_ref.at[pl.ds(pl.multiple_of(dst, STEP), STEP), :],
            sem,
        ).start()

    def of_candidate(c, at):
        n = blocks_of(len_ref[c])

        def body(i, carry):
            copy(c * length + i * STEP, (at + i) * STEP)
            return carry

        lax.fori_loop(0, n, body, 0)
        return at + n

    used = lax.fori_loop(0, count, of_candidate, 0)

    def pad(i, carry):
        copy(0, i * STEP)
        return carry

    lax.fori_loop(used, T // STEP, pad, 0)
    pltpu.make_async_copy(all_ref.at[pl.ds(0, T), :], out_ref, sem).wait()


def compact(tokens, cand_len, T):
    return pl.pallas_call(
        compact_kernel,
        out_shape=jax.ShapeDtypeStruct((T, tokens.shape[1]), tokens.dtype),
        in_specs=[pl.BlockSpec(memory_space=pltpu.SMEM), pl.BlockSpec(memory_space=pl.ANY)],
        out_specs=pl.BlockSpec(memory_space=pltpu.VMEM),
        scratch_shapes=[pltpu.SemaphoreType.DMA],
        compiler_params=pltpu.CompilerParams(vmem_limit_bytes=32 * 2**20),
        name="compact_tokens",
    )(cand_len, tokens)


def expand_kernel(len_ref, pairs_ref, all_ref, out_ref, buf, sem):
    w = lax.axis_index("wide")
    rows = out_ref.shape[0]
    count = len_ref.shape[0]
    last = all_ref.shape[0] // STEP - 1
    length = rows * lax.axis_size("wide") // (2 * count)
    first = w * rows
    pair, half, place = first // (2 * length), first // length % 2, first % length
    cand = pairs_ref[pair, half]

    def before(c, at):
        return at + jnp.where(c < cand, blocks_of(len_ref[c]), 0)

    start = lax.fori_loop(0, count, before, 0) + place // STEP

    def body(i, carry):
        src = jnp.minimum(start + i, last)
        pltpu.make_async_copy(
            all_ref.at[pl.ds(pl.multiple_of(src * STEP, STEP), STEP), :],
            buf.at[pl.ds(pl.multiple_of(i * STEP, STEP), STEP), :],
            sem,
        ).start()
        return carry

    lax.fori_loop(0, rows // STEP, body, 0)
    pltpu.make_async_copy(all_ref.at[pl.ds(0, rows), :], buf, sem).wait()
    live = len_ref[cand] - place

    def mask(i, carry):
        at = pl.ds(pl.multiple_of(i * STEP, STEP), STEP)
        row = i * STEP + lax.broadcasted_iota(jnp.int32, (STEP, out_ref.shape[1]), 0)
        out_ref[at, :] = jnp.where(row < live, buf[at, :].astype(F32), 0.0).astype(BF16)
        return carry

    lax.fori_loop(0, rows // STEP, mask, 0)


def expand(compacted, cand_len, pairs, rows):
    return pl.pallas_call(
        expand_kernel,
        out_shape=jax.ShapeDtypeStruct((rows, compacted.shape[1]), BF16),
        in_specs=[
            pl.BlockSpec(memory_space=pltpu.SMEM),
            pl.BlockSpec(memory_space=pltpu.SMEM),
            pl.BlockSpec(memory_space=pl.ANY),
        ],
        out_specs=pl.BlockSpec(memory_space=pltpu.VMEM),
        scratch_shapes=[pltpu.VMEM((rows, compacted.shape[1]), BF16), pltpu.SemaphoreType.DMA],
        name="expand_outputs",
    )(cand_len, pairs, compacted)


D = 8192
epsilon = 1e-06
BUCKETS = (1280, 1408, 1536, 2048)


def local(cand, norm_gain, gate_weight, up_weight, down_weight, pairs, cand_len):
    values = cand.astype(F32)
    squares = lax.psum(jnp.sum(values * values, axis=1), "narrow")
    normed = (values * lax.rsqrt(squares / D + epsilon)[:, None] * norm_gain[None, :]).astype(BF16)
    tokens = gather_wide(normed)
    blank = jnp.zeros((36, cand.shape[1]), BF16)
    tail = jnp.concatenate([gate_weight[896:], blank, up_weight[896:], blank])
    down_tail = jnp.concatenate([down_weight[896:], jnp.zeros((100, cand.shape[1]), BF16)])
    rows = 2 * tokens.shape[0] // lax.axis_size("wide")

    def branch(i, T):
        def run(tokens):
            x = compact(tokens, cand_len, T)
            hid = hidden_units(x, gate_weight, up_weight, tail, 1 + 2 * i)
            out = outputs(hid, down_weight, down_tail, 2 + 2 * i)
            return expand(out, cand_len, pairs, rows)

        return run

    used = jnp.sum(blocks_of(cand_len)) * STEP
    bucket = jnp.sum((used > jnp.array(BUCKETS[:-1], jnp.int32)).astype(jnp.int32))
    return lax.switch(bucket, [branch(i, T) for i, T in enumerate(BUCKETS)], tokens)


def solution(mesh):
    return jax.shard_map(
        local,
        mesh=mesh,
        in_specs=(
            P("wide", "narrow"),
            P("narrow"),
            P("wide", "narrow"),
            P("wide", "narrow"),
            P("wide", "narrow"),
            P(),
            P(),
        ),
        out_specs=P("wide", "narrow"),
        check_vma=False,
    )
```

time: 699 us -> 213 us (0.30)
  waiting for transfers between devices: 617 us -> 0 us
  Pallas kernels: 0 us -> 193 us
  matrix products: 42.6 us -> 0 us
  between operations: 13.5 us -> 1.39 us
    reduce_scatter x3 -> x0, waiting for transfers between devices: 360 us -> none  [the longest x1 226 us: local(): lax.psum_scatter(terms * live.reshape(cand_tokens)[:, None], 'wide', scat...]
    all_gather x3 -> x0, waiting for transfers between devices: 256 us -> none  [the longest x1 111 us: local(): gathered = lax.all_gather(cand, 'wide', axis=0, tiled=True)]
    pallas_call x0 -> x5, Pallas kernels: none -> 193 us  [the longest x1 77.6 us: outputs(): pl.pallas_call(functools.partial(output_kernel, names), out_shape=jax.Sha...]
    dot_general x3 -> x0, matrix products: 42.6 us -> none  [the longest x1 15.1 us: local(): lax.dot_general(lax.all_gather(hidden, 'narrow', axis=1, tiled=True), dow...]
    gather x2 -> x0, local copies, waits for them, and re-layouts: 8.2 us -> none  [the longest x1 6.69 us: local(): result = spread[source]]
  transfers between devices with their start and end apart: 6 -> 0, of which waited for: 6 -> 0; matrix products, arithmetic and copies ran while one was open for 2% -> 0% of each run, Pallas kernels for 0% -> 0%
where the time goes in v1:
time: 213 us; the launch traced here: 212 us
  Pallas kernels  193 us (91%)
  blocking collectives  7.41 us (3%)
  local copies, waits for them, and re-layouts  5.62 us (3%)
  other arithmetic  4.29 us (2%)
    pallas_call x1, Pallas kernels, outputs(): pl.pallas_call(functools.partial(output_kernel, names), out_shape=jax.Sha...  77.6 us
    pallas_call x1, Pallas kernels, hidden_units(): pl.pallas_call(hidden_kernel, out_shape=jax.ShapeDtypeStruct((T, 1024), B...  55.6 us
    pallas_call x1, Pallas kernels, gather_wide(): pl.pallas_call(gather_kernel, out_shape=jax.ShapeDtypeStruct((2, 4, 4, ro...  54.3 us
    psum x1, blocking collectives, local(): squares = lax.psum(jnp.sum(values * values, axis=1), 'narrow')  7.41 us

profile of v1, /device:TPU:0, one launch (start us, length us, event | category | flops | bytes accessed | tf_op | source)
XLA Modules:
  0.0 212.2 jit_solution(9208760059924441580)
XLA Ops:
  0.0 0.0 slice-start.1
  0.0 0.0 slice-start
  0.0 1.1 fusion
  1.2 7.4 %psum.7 = f32[64]{0:T(128)S(1)} all-reduce(f32[64]{0:T(128)S(1)} %fusion), channel_id=1, replica_groups=mesh['narrow'=4,'wide'=32] {'narrow'}, use_global_device_ids=true, to_apply=%region_3.4 | all-reduce | flops 64 | bytes 512 | tf_op jit(solution)/shard_map/psum | solution.py:679
  8.6 1.8 fusion.2.own_ref
  10.4 0.0 copy-start.5
  10.4 0.0 copy-start.7
  10.4 0.0 copy-start.6
  10.4 54.3 %gather_tokens.1 = bf16[2,4,4,64,2048]{4,3,2,1,0:T(8,128)(2,1)} custom-call(bf16[64,2048]{1,0:T(8,128)(2,1)} %fusion.2.own_ref), custom_call_target="tpu_custom_call" | custom-call | tf_op jit(solution)/shard_map/gather_tokens/pallas_call | solution.py:163
  64.7 0.0 slice-done.1
  64.7 0.0 slice-done
  64.7 0.1 pad_maximum_fusion
  64.8 0.0 copy-done.5
  64.8 0.6 fusion.4
  66.1 0.0 copy-done.7
  66.1 0.6 fusion.3
  66.8 0.0 copy-done.6
  67.4 144.0 %conditional.1 = (bf16[128,2048]{1,0:T(8,128)(2,1)S(1)}) conditional(s32[]{:T(128)} %clamp.3, (s32[8]{0:T(128)S(1)}, bf16[2,4,4,64,2048]{4,3,2,1,0:T(8,128)(2,1)}, bf16[924,2048]{1,0:T(8,128)(2,1)}, bf16[924,2048]{1,0:T(8,128)(2,1)}, bf16[128,2048]{1,0:T(8,128)(2,1)S(1)}, /*index=5*/bf16[924,2048]{1,0:T(8,128)(2,1)}, ...), branch_computations={%region_4.5_spmd, %region_5.6_spmd, %region_6.7_spmd, %region_7.8_... | conditional | bytes 34422952 | solution.py:698
  67.4 3.3 %compact_tokens.4.x_ref = bf16[1280,2048]{1,0:T(8,128)(2,1)S(1)} custom-call(s32[8]{0:T(128)S(1)} %get-tuple-element.72.len_ref, bf16[2048,2048]{1,0:T(8,128)(2,1)} %bitcast.4), custom_call_target="tpu_custom_call" | custom-call | tf_op jit(solution)/shard_map/cond/branch_0_fun/compact_tokens/pallas_call | solution.py:609
  70.8 0.0 copy-start.3
  70.8 2.4 %copy-done.3 = bf16[1280,2048]{1,0:T(8,128)(2,1)} copy-done((bf16[1280,2048]{1,0:T(8,128)(2,1)}, bf16[1280,2048]{1,0:T(8,128)(2,1)S(1)}, u32[]{:S(2)}) %copy-start.3) | copy-done | bytes 5242904 | tf_op jit(solution)/shard_map/cond
  73.1 55.6 %hidden_units.4.hid_ref = bf16[1280,1024]{1,0:T(8,128)(2,1)} custom-call(bf16[1280,2048]{1,0:T(8,128)(2,1)} %copy-done.3, bf16[924,2048]{1,0:T(8,128)(2,1)} %get-tuple-element.77.gate_ref, bf16[924,2048]{1,0:T(8,128)(2,1)} %get-tuple-element.78.up_ref, bf16[128,2048]{1,0:T(8,128)(2,1)S(1)} %get-tuple-element.79.tail_ref), custom_call_target="tpu_custom_call" | custom-call | tf_op jit(solution)/shard_map/cond/branch_0_fun/hidden_units/pallas_call | solution.py:463
  128.7 0.9 slice.12
  129.7 0.8 concatenate.8.tail_ref
  130.5 77.6 %reduce_outputs.4.all_ref = bf16[1280,2048]{1,0:T(8,128)(2,1)} custom-call(bf16[1280,1024]{1,0:T(8,128)(2,1)} %hidden_units.4.hid_ref, bf16[924,2048]{1,0:T(8,128)(2,1)} %get-tuple-element.123, bf16[128,2048]{1,0:T(8,128)(2,1)} %concatenate.8.tail_ref), custom_call_target="tpu_custom_call" | custom-call | tf_op jit(solution)/shard_map/cond/branch_0_fun/reduce_outputs/pallas_call | solution.py:545
  208.1 0.7 copy.17.pairs_ref
  208.8 2.1 expand_outputs.4
  211.4 0.0 copy-start.4
  211.4 0.8 copy-done.4
  (2 shorter events, 0.0 us)
Async XLA Ops:
  0.0 64.7 %slice-start.1 = ((bf16[924,2048]{1,0:T(8,128)(2,1)}), bf16[28,2048]{1,0:T(8,128)(2,1)S(1)}, s32[]{:S(2)}) async-start(bf16[924,2048]{1,0:T(8,128)(2,1)} %param.15), calls=%async_computation.1 | async-start | bytes 262144 | tf_op jit(solution)/shard_map/slice | solution.py:683
  0.0 64.7 %slice-start = ((bf16[924,2048]{1,0:T(8,128)(2,1)}), bf16[28,2048]{1,0:T(8,128)(2,1)S(1)}, s32[]{:S(2)}) async-start(bf16[924,2048]{1,0:T(8,128)(2,1)} %param.14), calls=%async_computation | async-start | bytes 262144 | tf_op jit(solution)/shard_map/slice | solution.py:683
  10.4 54.5 %copy-start.5 = (s32[8]{0:T(128)S(1)}, s32[8]{0:T(128)}, u32[]{:S(2)}) copy-start(s32[8]{0:T(128)} %param.18) | copy-start | bytes 100
  10.4 55.8 %copy-start.7 = (s32[3]{0:T(128)S(1)}, s32[3]{0:T(128)}, u32[]{:S(2)}) copy-start(s32[3]{0:T(128)} %constant.36.clone) | copy-start | bytes 40
  10.4 56.4 %copy-start.6 = (s32[8,2]{0,1:T(2,128)S(1)}, s32[8,2]{0,1:T(2,128)}, u32[]{:S(2)}) copy-start(s32[8,2]{0,1:T(2,128)} %param.17) | copy-start | bytes 196
  70.8 2.4 %copy-start.3 = (bf16[1280,2048]{1,0:T(8,128)(2,1)}, bf16[1280,2048]{1,0:T(8,128)(2,1)S(1)}, u32[]{:S(2)}) copy-start(bf16[1280,2048]{1,0:T(8,128)(2,1)S(1)} %compact_tokens.4.x_ref) | copy-start | bytes 15728644 | tf_op jit(solution)/shard_map/cond
  211.4 0.8 copy-start.4

commit v2 on v0

v2 whole, which is shorter than its diff:
```python
import functools

import jax
import jax.numpy as jnp
from jax import lax
from jax.experimental import pallas as pl
from jax.experimental.pallas import tpu as pltpu
from jax.sharding import PartitionSpec as P

MESH = pl.DeviceIdType.MESH
F32 = jnp.float32
BF16 = jnp.bfloat16


class Net:
    def __init__(self, send_sem, recv_sem):
        self.send_sem, self.recv_sem = send_sem, recv_sem
        self.index, self.sent = {}, []

    def slot(self, key):
        return self.index.setdefault(key, len(self.index))

    def send(self, key, src, dst, device):
        i = self.slot(key)
        copy = pltpu.make_async_remote_copy(
            src_ref=src, dst_ref=dst, send_sem=self.send_sem.at[i], recv_sem=self.recv_sem.at[i],
            device_id=device, device_id_type=MESH,
        )
        copy.start()
        self.sent.append(copy)
        return copy

    def recv(self, key, dst, device):
        i = self.slot(key)
        pltpu.make_async_remote_copy(
            src_ref=dst, dst_ref=dst, send_sem=self.send_sem.at[i], recv_sem=self.recv_sem.at[i],
            device_id=device, device_id_type=MESH,
        ).wait_recv()

    def finish(self):
        for copy in self.sent:
            copy.wait_send()
        self.sent = []


def position():
    w = lax.axis_index("wide")
    return w // 16, (w // 4) % 4, w % 4


def wide_of(c, z, p, q):
    x, y = (p, q) if c == 0 else (q, p)
    return {"wide": z * 16 + ((x + 8) % 4) * 4 + (y + 8) % 4}


def coords(c, x, y):
    return (x, y) if c == 0 else (y, x)


def mod4(a):
    return (a + 8) % 4


def all_gather_wide(net, tag, reg, reg2):
    z, x, y = position()
    pq = [coords(0, x, y), coords(1, x, y)]
    half = {1: 0, -1: 1}

    def r1(c, zz, p, q):
        a, b = coords(c, mod4(p), mod4(q))
        return reg(c, zz, a, b)

    def r2(c, p, q):
        a, b = coords(c, mod4(p), mod4(q))
        return reg2(c, a, b)

    def send(key, region, c, dz, p, q):
        net.send((tag,) + key, region, region, wide_of(c, dz, p, q))

    def recv(key, region, c):
        net.recv((tag,) + key, region, wide_of(c, z, x, y))

    def begin():
        for c in (0, 1):
            p, q = pq[c]
            send(("z", c), r1(c, z, p, q), c, 1 - z, p, q)
        for s in (1, -1):
            for c in (0, 1):
                p, q = pq[c]
                send(("p1", c, s, 0), r1(c, z, p, q), c, z, p + s, q)

    def other():
        for c in (0, 1):
            p, q = pq[c]
            recv(("z", c), r1(c, 1 - z, p, q), c)
            for s in (1, -1):
                send(("p1", c, s, 1), r1(c, 1 - z, p, q), c, z, p + s, q)
        for c in (0, 1):
            p, q = pq[c]
            for s in (1, -1):
                send(("q1", c, s, 0), r2(c, p, q), c, z, p, q + s)

    def near():
        for s in (1, -1):
            for c in (0, 1):
                p, q = pq[c]
                recv(("p1", c, s, 0), r1(c, z, p - s, q), c)
                recv(("p1", c, s, 1), r1(c, 1 - z, p - s, q), c)
                send(("p2", c, s), r1(c, half[s], p - s, q), c, z, p + s, q)
        for s in (1, -1):
            for c in (0, 1):
                p, q = pq[c]
                for t in (1, -1):
                    send(("q1", c, t, -s), r2(c, p - s, q), c, z, p, q + t)

    def opposite():
        for c in (0, 1):
            p, q = pq[c]
            for s in (1, -1):
                recv(("p2", c, s), r1(c, half[s], p - 2 * s, q), c)
            for t in (1, -1):
                send(("q1", c, t, 2), r2(c, p + 2, q), c, z, p, q + t)

    def forward(rel):
        def run():
            for s in (1, -1):
                for c in (0, 1):
                    p, q = pq[c]
                    recv(("q1", c, s, rel), r2(c, p + rel, q - s), c)
                    send(("q2", c, s, rel), r1(c, half[s], p + rel, q - s), c, z, p, q + s)

        return run

    def last():
        for rel in (0, -1, 1, 2):
            for s in (1, -1):
                for c in (0, 1):
                    p, q = pq[c]
                    recv(("q2", c, s, rel), r1(c, half[s], p + rel, q - 2 * s), c)

    return [begin, other, near, opposite] + [forward(rel) for rel in (0, -1, 1, 2)] + [last]


AG_MESSAGES = 2 * (1 + 4 + 2 + 8 + 8)


def add_rows(dst, srcs, rows, step=16):
    def body(i, carry):
        at = pl.ds(pl.multiple_of(i * step, step), step)
        total = srcs[0][at, :].astype(F32)
        for src in srcs[1:]:
            total = total + src[at, :].astype(F32)
        dst[at, :] = total.astype(dst.dtype)
        return carry

    lax.fori_loop(0, rows // step, body, 0)


def reduce_ring(net, tag, c, axis, unit, bufs):
    z, x, y = position()
    p, q = coords(c, x, y)
    me = p if axis == "p" else q
    r1, r2, sb = bufs
    rows, cols = r2.shape[1:]
    hc = cols // 2
    half = {1: 0, -1: 1}

    def dev(s):
        return wide_of(c, z, p + s, q) if axis == "p" else wide_of(c, z, p, q + s)

    def part(ref, h):
        return ref.at[:, pl.ds(h * hc, hc)]

    def first():
        for s in (1, -1):
            net.send((tag, "r1", c, s), part(unit(mod4(me + 2)), half[s]), r1.at[half[s]], dev(s))

    def direct():
        for s in (1, -1):
            o = 1 - half[s]
            net.send((tag, "r2d", c, s), part(unit(mod4(me + s)), o), part(r2.at[half[s]], o), dev(s))

    def middle():
        for s in (1, -1):
            h = half[s]
            net.recv((tag, "r1", c, s), r1.at[h], dev(s))
            add_rows(sb.at[h], [part(unit(mod4(me + s)), h), r1.at[h]], rows)
            net.send((tag, "r2s", c, s), sb.at[h], part(r2.at[h], h), dev(s))

    def end(dst):
        for s in (1, -1):
            h = half[s]
            net.recv((tag, "r2d", c, s), part(r2.at[h], 1 - h), dev(s))
            net.recv((tag, "r2s", c, s), part(r2.at[h], h), dev(s))
        add_rows(dst, [unit(mod4(me)), r2.at[0], r2.at[1]], rows)

    return first, direct, middle, end


def reduce_scatter_wide(net, tag, part_ref, bufs, dst, tiles):
    z, x, y = position()
    H = part_ref.shape[0]
    C = part_ref.shape[1] // 2
    K = C // 4
    Q = [bufs["q0"], bufs["q1"]]

    def big(c):
        return lambda j: part_ref.at[:, pl.ds(pl.multiple_of(c * C + j * K, 128), K)]

    def small(c):
        return lambda j: Q[c].at[pl.ds(pl.multiple_of(j * (H // 4), 16), H // 4), :]

    one = [reduce_ring(net, tag + "a", c, "q", big(c), [bufs[f"{k}{c}"] for k in ("ra", "rb", "sa")]) for c in (0, 1)]
    two = [reduce_ring(net, tag + "b", c, "p", small(c), [bufs[f"{k}{c}"] for k in ("rc", "rd", "sc")]) for c in (0, 1)]

    def side(c, zz):
        return bufs[f"w{c}"].at[:, pl.ds(pl.multiple_of(zz * (K // 2), 128), K // 2)]

    def far():
        tiles(2)
        for c in (0, 1):
            one[c][0]()

    def near():
        tiles(1, -1)
        for c in (0, 1):
            one[c][1]()

    def middle():
        for c in (0, 1):
            one[c][2]()

    def own():
        tiles(0)

    def turn():
        for c in (0, 1):
            one[c][3](Q[c])
            two[c][0]()
            two[c][1]()

    def middle2():
        for c in (0, 1):
            two[c][2]()

    def across():
        for c in (0, 1):
            two[c][3](bufs[f"w{c}"])
            p, q = coords(c, x, y)
            net.send((tag + "c", c), side(c, 1 - z), bufs[f"v{c}"], wide_of(c, 1 - z, p, q))

    def last():
        for c in (0, 1):
            p, q = coords(c, x, y)
            net.recv((tag + "c", c), bufs[f"v{c}"], wide_of(c, 1 - z, p, q))
            add_rows(dst(c), [side(c, z), bufs[f"v{c}"]], H // 4)

    return [far, near, middle, own, turn, middle2, across, last]


RS_MESSAGES = 2 * (6 + 6 + 1)


def reduce_bufs(H, C):
    K = C // 4
    shapes = {}
    for c, (rows, cols) in enumerate(((H, K), (H, K))):
        shapes[f"q{c}"] = (rows, cols)
        shapes[f"ra{c}"] = (2, rows, cols // 2)
        shapes[f"rb{c}"] = (2, rows, cols)
        shapes[f"sa{c}"] = (2, rows, cols // 2)
        shapes[f"rc{c}"] = (2, H // 4, K // 2)
        shapes[f"rd{c}"] = (2, H // 4, K)
        shapes[f"sc{c}"] = (2, H // 4, K // 2)
        shapes[f"w{c}"] = (H // 4, K)
        shapes[f"v{c}"] = (H // 4, K // 2)
    shapes["res"] = (2, H // 4, K // 2)
    return shapes


STEP = 16


def blocks_of(length):
    return (length + STEP - 1) // STEP


D = 8192
epsilon = 1e-06
TILES = 8
PAIRS_OF = 5


def barrier():
    z, x, y = position()
    n = lax.axis_index("narrow")
    sem = pltpu.get_barrier_semaphore()
    partners = [
        wide_of(0, z, x + 1, y), wide_of(0, z, x - 1, y),
        wide_of(0, z, x, y + 1), wide_of(0, z, x, y - 1), wide_of(0, 1 - z, x, y),
    ] + [{"narrow": dev} for dev in narrow_peers()]
    for dev in partners:
        pl.semaphore_signal(sem, inc=1, device_id=dev, device_id_type=MESH)
    pl.semaphore_wait(sem, len(partners))


def narrow_peers():
    n = lax.axis_index("narrow")
    zl, co = n // 2, n % 2
    return zl * 2 + 1 - co, (1 - zl) * 2 + co, (1 - zl) * 2 + 1 - co


def load_weights(gate_ref, up_ref, down_ref, w_ref, d_ref, t_ref, sem):
    loads = []
    for k in range(3):
        loads.append((gate_ref.at[pl.ds(k * 256, 256), :], w_ref.at[pl.ds(k * 512, 256), :]))
        loads.append((up_ref.at[pl.ds(k * 256, 256), :], w_ref.at[pl.ds(k * 512 + 256, 256), :]))
    loads.append((gate_ref.at[pl.ds(768, 128), :], w_ref.at[pl.ds(1536, 128), :]))
    loads.append((up_ref.at[pl.ds(768, 128), :], w_ref.at[pl.ds(1664, 128), :]))
    loads.append((down_ref.at[pl.ds(0, 896), :], d_ref.at[pl.ds(0, 896), :]))
    for k, ref in enumerate((gate_ref, up_ref, down_ref)):
        loads.append((ref.at[pl.ds(896, 28), :], t_ref[k]))
    return [pltpu.make_async_copy(s, d, sem.at[i]) for i, (s, d) in enumerate(loads)]


def place_tails(w_ref, d_ref, t_ref):
    cols = d_ref.shape[1]
    blank = jnp.zeros((16, cols), BF16)
    for k, (ref, at, rows) in enumerate(((w_ref, 1792, 64), (w_ref, 1856, 64), (d_ref, 896, 128))):
        ref[pl.ds(at, 16), :] = t_ref[k][pl.ds(0, 16), :]
        ref[pl.ds(at + 16, 16), :] = jnp.concatenate([t_ref[k][pl.ds(16, 12), :], jnp.zeros((4, cols), BF16)])
        for i in range(2, rows // 16):
            ref[pl.ds(at + i * 16, 16), :] = blank


def normalise(cand_ref, gain_ref, own, square_ref, peers_ref, send_sem, recv_sem):
    rows, cols = cand_ref.shape

    def squares(i, carry):
        at = pl.ds(pl.multiple_of(i * 16, 16), 16)
        v = cand_ref[at, :].astype(F32)
        square_ref[at, :] = jnp.broadcast_to(jnp.sum(v * v, axis=1, keepdims=True), (16, 128))
        return carry

    lax.fori_loop(0, rows // 16, squares, 0)
    copies = [
        pltpu.make_async_remote_copy(
            src_ref=square_ref, dst_ref=peers_ref.at[k], send_sem=send_sem.at[k], recv_sem=recv_sem.at[k],
            device_id={"narrow": dev}, device_id_type=MESH,
        )
        for k, dev in enumerate(narrow_peers())
    ]
    barrier()
    for copy in copies:
        copy.start()
    for copy in copies:
        copy.wait()

    def scale(i, carry):
        at = pl.ds(pl.multiple_of(i * 16, 16), 16)
        total = square_ref[at, :] + peers_ref[0, at, :] + (peers_ref[1, at, :] + peers_ref[2, at, :])
        inv = lax.rsqrt(total[:, :1] / D + epsilon)
        own[i] = (cand_ref[at, :].astype(F32) * inv * gain_ref[...]).astype(BF16)
        return carry

    lax.fori_loop(0, rows // 16, scale, 0)


def compact(source_ref, all_ref, x_ref, h):
    H = x_ref.shape[0]
    M = H // 4
    n = lax.axis_index("narrow")
    core, far, both = narrow_peers()
    for k, dev in enumerate((both, far, core, n)):

        def body(i, carry, k=k, dev=dev):
            j = (h * H + dev * M) // STEP + i
            x_ref[pl.ds(pl.multiple_of(k * M + i * STEP, STEP), STEP), :] = all_ref[source_ref[0, j], source_ref[1, j]]
            return carry

        lax.fori_loop(0, M // STEP, body, 0)


def hidden_flow(x_ref, w_ref, hid_ref, z_ref, bufs):
    n = lax.axis_index("narrow")
    core, far, both = narrow_peers()
    H = x_ref.shape[0]
    M = H // 4
    own_ref, sa, ra, sz, rz, sb, rb, sems = bufs
    a_send, a_recv, z_send, z_recv, b_send, b_recv, hc_send, hc_recv, hz_send, hz_recv, hf_send, hf_recv = sems

    def link(src, dst, send, recv, device):
        return pltpu.make_async_remote_copy(
            src_ref=src, dst_ref=dst, send_sem=send, recv_sem=recv, device_id={"narrow": device}, device_id_type=MESH
        )

    def cut(ref, at, width):
        return ref.at[:, pl.ds(at, width)]

    def product(j, at, width):
        value = lax.dot_general(
            x_ref[...], w_ref[pl.ds(at, width), :], (((1,), (1,)), ((), ())), preferred_element_type=F32
        )
        cut(sa, at, width)[...] = value[:M].astype(BF16)
        cut(z_ref, at, width)[...] = value[M:2 * M]
        cut(sb, at, width)[...] = value[2 * M:3 * M].astype(BF16)
        cut(own_ref, at, width)[...] = value[3 * M:]
        link(cut(sa, at, width), cut(ra, at, width), a_send.at[j], a_recv.at[j], core).start()
        link(cut(sb, at, width), cut(rb, at, width), b_send.at[j], b_recv.at[j], core).start()

    def to_far(j, at, width):
        link(cut(sz, at, width), cut(rz, at, width), z_send.at[j], z_recv.at[j], far).start()

    def combine(j, at, width, held):
        link(cut(ra, at, width), cut(ra, at, width), a_send.at[j], a_recv.at[j], core).wait_recv()
        cut(sz, at, width)[...] = (cut(z_ref, at, width)[...] + cut(ra, at, width)[...].astype(F32)).astype(BF16)
        if held:
            @pl.when(j >= held)
            def _():
                to_far(j, at, width)
        else:
            to_far(j, at, width)
        link(cut(rb, at, width), cut(rb, at, width), b_send.at[j], b_recv.at[j], core).wait_recv()
        cut(own_ref, at, width)[...] = cut(own_ref, at, width)[...] + cut(rb, at, width)[...].astype(F32)

    def multiply(held=0, between=None):
        def body(j, carry):
            at = pl.multiple_of(j * 256, 256)
            product(j, at, 256)

            @pl.when(j >= 1)
            def _():
                combine(j - 1, pl.multiple_of(at - 256, 256), 256, held)

            if held:
                @pl.when(j == held)
                def _():
                    between()
                    for k in range(held):
                        to_far(k, k * 256, 256)
            return carry

        lax.fori_loop(0, 7, body, 0)
        product(7, 1792, 128)
        combine(6, 1536, 256, 0)
        combine(7, 1792, 128, 0)

    def await_far(j, at, width):
        link(cut(rz, at, width), cut(rz, at, width), z_send.at[j], z_recv.at[j], far).wait_recv()

    def total(at, width, r):
        return own_ref[r, pl.ds(at, width)] + rz[r, pl.ds(at, width)].astype(F32)

    def gated(g, u):
        return (g / (1.0 + jnp.exp(-g)) * u).astype(BF16)

    def hid(block, at, width):
        return hid_ref.at[pl.ds(pl.multiple_of(block * M, 16), M), pl.ds(at, width)]

    def over_rows(at, width, value):
        def body(i, carry):
            rows = pl.ds(pl.multiple_of(n * M + i * 16, 16), 16)
            hid_ref[rows, pl.ds(at, width)] = value(pl.ds(pl.multiple_of(i * 16, 16), 16))
            return carry

        lax.fori_loop(0, M // 16, body, 0)

    def spread(k, at, width):
        mine = hid(n, at, width)
        link(mine, mine, hz_send.at[k], hz_recv.at[k], far).start()
        link(mine, mine, hc_send.at[k], hc_recv.at[k], core).start()

    def finish():
        def pair(k, carry):
            g, u, h = (pl.multiple_of(v, 256) for v in (k * 512, k * 512 + 256, k * 256))
            await_far(2 * k, g, 256)
            await_far(2 * k + 1, u, 256)
            over_rows(h, 256, lambda r: gated(total(g, 256, r), total(u, 256, r)))
            spread(k, h, 256)
            return carry

        lax.fori_loop(0, 3, pair, 0)
        await_far(6, 1536, 256)
        over_rows(768, 128, lambda r: gated(total(1536, 128, r), total(1664, 128, r)))
        spread(3, 768, 128)
        await_far(7, 1792, 128)

        def last(r):
            g = total(1792, 128, r)
            return gated(g, pltpu.roll(g, 64, 1))

        over_rows(896, 128, last)
        spread(4, 896, 128)

    cols = [(k, k * 256, 256) for k in range(3)] + [(3, 768, 128), (4, 896, 128)]

    def collect():
        for k, at, width in cols:
            theirs = hid(far, at, width)
            link(theirs, theirs, hz_send.at[k], hz_recv.at[k], far).wait_recv()
            link(theirs, theirs, hf_send.at[k], hf_recv.at[k], core).start()
        for k, at, width in cols:
            theirs = hid(core, at, width)
            link(theirs, theirs, hc_send.at[k], hc_recv.at[k], core).wait_recv()
        for k, at, width in cols:
            theirs = hid(both, at, width)
            link(theirs, theirs, hf_send.at[k], hf_recv.at[k], core).wait_recv()

    def drain():
        for j in range(TILES):
            at, width = j * 256, (256 if j < 7 else 128)
            for s, send, recv in ((sa, a_send, a_recv), (sz, z_send, z_recv), (sb, b_send, b_recv)):
                link(cut(s, at, width), cut(s, at, width), send.at[j], recv.at[j], core).wait_send()
        for k, at, width in cols:
            mine = hid(n, at, width)
            link(mine, mine, hz_send.at[k], hz_recv.at[k], far).wait_send()
            link(mine, mine, hc_send.at[k], hc_recv.at[k], core).wait_send()
            theirs = hid(far, at, width)
            link(theirs, theirs, hf_send.at[k], hf_recv.at[k], core).wait_send()

    return dict(multiply=multiply, finish=finish, collect=collect, drain=drain)


def output_tiles(hid_ref, d_ref, part_ref):
    z, x, y = position()

    def tiles(*steps):
        def body(i, carry):
            step = steps[0] if len(steps) == 1 else jnp.where(i < 2, steps[0], steps[1])
            k = jnp.where(i % 2 == 0, mod4(y + step), 4 + mod4(x + step))
            at = pl.ds(pl.multiple_of(k * 256, 256), 256)
            part_ref[:, at] = jnp.dot(hid_ref[...], d_ref[:, at], preferred_element_type=F32).astype(BF16)
            return carry

        lax.fori_loop(0, 2 * len(steps), body, 0)

    return tiles


def feed_forward_kernel(names, source_ref, cand_ref, gain_ref, gate_ref, up_ref, down_ref, out_ref, *scratch):
    T = out_ref.shape[0]
    H = T // 2
    (all_ref, x_ref, w_ref, d_ref, hid_ref, z_ref, square_ref, peers_ref,
     w_sem, sq_send, sq_recv, copy_sem, send_sem, recv_sem) = scratch[:14]
    t_ref = scratch[14:17]
    scratch = scratch[17:]
    n_hid, n_sem, n_red = 7, 12, len(names)
    z, x, y = position()
    loads = load_weights(gate_ref, up_ref, down_ref, w_ref, d_ref, t_ref, w_sem)
    for copy in loads:
        copy.start()
    R, cols = cand_ref.shape
    C = cols // 2
    K = C // 4
    net = Net(send_sem, recv_sem)

    def place_of(a, b):
        return pl.ds((a * 4 + b) * (R // STEP), R // STEP)

    normalise(cand_ref, gain_ref, all_ref.at[z, place_of(x, y)], square_ref, peers_ref, sq_send, sq_recv)
    tokens = all_gather_wide(
        net, "t",
        lambda c, zz, a, b: all_ref.at[zz, place_of(a, b), :, pl.ds(c * C, C)],
        lambda c, a, b: all_ref.at[:, place_of(a, b), :, pl.ds(c * C, C)],
    )
    for stage in tokens[:2]:
        stage()
    for copy in loads:
        copy.wait()
    place_tails(w_ref, d_ref, t_ref)
    for stage in tokens[2:]:
        stage()

    hidden, reduce, gather = [], [], []
    for h in (0, 1):
        mine = scratch[h * (n_hid + n_sem + n_red):(h + 1) * (n_hid + n_sem + n_red)]
        bufs = dict(zip(names, mine[n_hid + n_sem:]))
        hid, part = hid_ref.at[pl.ds(h * H, H), :], x_ref.at[h]
        hidden.append(hidden_flow(x_ref.at[h], w_ref, hid, z_ref, mine[:n_hid] + (mine[n_hid:n_hid + n_sem],)))
        res = bufs["res"]

        def reg(c, zz, a, b, h=h):
            p, q = coords(c, a, b)
            return out_ref.at[
                pl.ds(pl.multiple_of(h * H + p * (H // 4), 16), H // 4),
                pl.ds(pl.multiple_of(c * C + q * K + zz * (K // 2), 128), K // 2),
            ]

        def reg2(c, a, b, h=h):
            p, q = coords(c, a, b)
            return out_ref.at[
                pl.ds(pl.multiple_of(h * H + p * (H // 4), 16), H // 4), pl.ds(pl.multiple_of(c * C + q * K, 128), K)
            ]

        stages = reduce_scatter_wide(
            net, f"r{h}", part, bufs, lambda c, res=res: res.at[c], output_tiles(hid, d_ref, part)
        )

        def place(last=stages.pop(), res=res, reg=reg, h=h):
            last()
            copies = [pltpu.make_async_copy(res.at[c], reg(c, z, x, y), copy_sem.at[h, c]) for c in (0, 1)]
            for copy in copies:
                copy.start()
            for copy in copies:
                copy.wait()

        reduce.append(stages + [place])
        gather.append(all_gather_wide(net, f"g{h}", reg, reg2))

    h0, h1 = hidden
    r0, r1 = reduce
    g0, g1 = gather
    compact(source_ref, all_ref, x_ref.at[0], 0)
    h0["multiply"]()
    compact(source_ref, all_ref, x_ref.at[1], 1)
    h1["multiply"](4, h0["finish"])
    h0["collect"]()
    for stage in r0[:4]:
        stage()
    h1["finish"]()
    for stage in r0[4:7]:
        stage()
    h1["collect"]()
    order = [r1[0], r0[7], g0[0], r1[1], g0[1], r1[2], r1[3], g0[2], g0[3], r1[4], g0[4], g0[5], r1[5], g0[6], g0[7], r1[6], g0[8], r1[7]]
    for stage in order + g1:
        stage()
    net.finish()
    h0["drain"]()
    h1["drain"]()


def feed_forward(source, cand, norm_gain, gate_weight, up_weight, down_weight, T, collective_id):
    R, cols = cand.shape
    W = lax.axis_size("wide")
    H = T // 2
    M, N = H // 4, 1920
    DMA, VMEM = pltpu.SemaphoreType.DMA, pltpu.VMEM
    shapes = reduce_bufs(H, cols // 2)
    names = tuple(shapes)
    n = 3 * AG_MESSAGES + 2 * RS_MESSAGES
    chunk = (
        [VMEM((M, N), F32)] + [VMEM((M, N), BF16)] * 6
        + [DMA((TILES,))] * 6 + [DMA((PAIRS_OF,))] * 6
        + [VMEM(shapes[k], BF16) for k in names]
    )
    anywhere = pl.BlockSpec(memory_space=pl.ANY)
    inside = pl.BlockSpec(memory_space=pltpu.VMEM)
    return pl.pallas_call(
        functools.partial(feed_forward_kernel, names),
        out_shape=jax.ShapeDtypeStruct((T, cols), BF16),
        in_specs=[pl.BlockSpec(memory_space=pltpu.SMEM), inside, inside] + [anywhere] * 3,
        out_specs=anywhere,
        scratch_shapes=[
            VMEM((2, W * R // STEP // 2, STEP, cols), BF16), VMEM((2, H, cols), BF16), VMEM((N, cols), BF16), VMEM((1024, cols), BF16),
            VMEM((T, 1024), BF16), VMEM((M, N), F32), VMEM((R, 128), F32), VMEM((3, R, 128), F32),
            DMA((12,)), DMA((3,)), DMA((3,)), DMA((2, 2)), DMA((n,)), DMA((n,)),
        ] + [VMEM((28, cols), BF16)] * 3 + chunk * 2,
        compiler_params=pltpu.CompilerParams(
            collective_id=collective_id, has_side_effects=True, vmem_limit_bytes=67043328
        ),
        name="feed_forward",
    )(source, cand, norm_gain.reshape(1, cols), gate_weight, up_weight, down_weight)


def expand_kernel(len_ref, pairs_ref, all_ref, out_ref, buf, sem):
    w = lax.axis_index("wide")
    rows = out_ref.shape[0]
    count = len_ref.shape[0]
    last = all_ref.shape[0] // STEP - 1
    length = rows * lax.axis_size("wide") // (2 * count)
    first = w * rows
    pair, half, place = first // (2 * length), first // length % 2, first % length
    cand = pairs_ref[pair, half]

    def before(c, at):
        return at + jnp.where(c < cand, blocks_of(len_ref[c]), 0)

    start = lax.fori_loop(0, count, before, 0) + place // STEP

    def body(i, carry):
        src = jnp.minimum(start + i, last)
        pltpu.make_async_copy(
            all_ref.at[pl.ds(pl.multiple_of(src * STEP, STEP), STEP), :],
            buf.at[pl.ds(pl.multiple_of(i * STEP, STEP), STEP), :],
            sem,
        ).start()
        return carry

    lax.fori_loop(0, rows // STEP, body, 0)
    pltpu.make_async_copy(all_ref.at[pl.ds(0, rows), :], buf, sem).wait()
    live = len_ref[cand] - place

    def mask(i, carry):
        at = pl.ds(pl.multiple_of(i * STEP, STEP), STEP)
        row = i * STEP + lax.broadcasted_iota(jnp.int32, (STEP, out_ref.shape[1]), 0)
        out_ref[at, :] = jnp.where(row < live, buf[at, :].astype(F32), 0.0).astype(BF16)
        return carry

    lax.fori_loop(0, rows // STEP, mask, 0)


def expand(compacted, cand_len, pairs, rows):
    return pl.pallas_call(
        expand_kernel,
        out_shape=jax.ShapeDtypeStruct((rows, compacted.shape[1]), BF16),
        in_specs=[
            pl.BlockSpec(memory_space=pltpu.SMEM),
            pl.BlockSpec(memory_space=pltpu.SMEM),
            pl.BlockSpec(memory_space=pl.ANY),
        ],
        out_specs=pl.BlockSpec(memory_space=pltpu.VMEM),
        scratch_shapes=[pltpu.VMEM((rows, compacted.shape[1]), BF16), pltpu.SemaphoreType.DMA],
        name="expand_outputs",
    )(cand_len, pairs, compacted)


BUCKETS = (1280, 1408, 2048)


def local(cand, norm_gain, gate_weight, up_weight, down_weight, pairs, cand_len):
    rows = 2 * cand.shape[0]

    def branch(i, T):
        def run(cand):
            out = feed_forward(source, cand, norm_gain, gate_weight, up_weight, down_weight, T, i)
            return expand(out, cand_len, pairs, rows)

        return run

    count = cand_len.shape[0]
    per = cand.shape[0] * lax.axis_size("wide") // (count * STEP)
    blocks = blocks_of(cand_len)
    order = jnp.arange(count, dtype=jnp.int32)
    ends = jnp.sum(jnp.where(order[None, :] <= order[:, None], blocks[None, :], 0), axis=1)
    at = jnp.arange(count * per, dtype=jnp.int32)
    block = at + jnp.sum(jnp.where(at[None, :] >= ends[:, None], per - blocks[:, None], 0), axis=0)
    block = jnp.minimum(block, count * per - 1)
    half = count * per // 2
    source = jnp.stack([block // half, block % half])
    used = jnp.sum(blocks) * STEP
    bucket = jnp.sum((used > jnp.array(BUCKETS[:-1], jnp.int32)).astype(jnp.int32))
    return lax.switch(bucket, [branch(i, T) for i, T in enumerate(BUCKETS)], cand)


def solution(mesh):
    return jax.shard_map(
        local,
        mesh=mesh,
        in_specs=(
            P("wide", "narrow"),
            P("narrow"),
            P("wide", "narrow"),
            P("wide", "narrow"),
            P("wide", "narrow"),
            P(),
            P(),
        ),
        out_specs=P("wide", "narrow"),
        check_vma=False,
    )
```

time: 699 us -> 187 us (0.27)
  waiting for transfers between devices: 617 us -> 0 us
  Pallas kernels: 0 us -> 180 us
  matrix products: 42.6 us -> 0 us
  between operations: 13.5 us -> 1.33 us
  other arithmetic: 10.6 us -> 3.35 us
    reduce_scatter x3 -> x0, waiting for transfers between devices: 360 us -> none  [the longest x1 226 us: local(): lax.psum_scatter(terms * live.reshape(cand_tokens)[:, None], 'wide', scat...]
    all_gather x3 -> x0, waiting for transfers between devices: 256 us -> none  [the longest x1 111 us: local(): gathered = lax.all_gather(cand, 'wide', axis=0, tiled=True)]
    pallas_call x0 -> x2, Pallas kernels: none -> 180 us  [the longest x1 178 us: feed_forward(): pl.pallas_call(functools.partial(feed_forward_kernel, names), out_shape=j...]
    dot_general x3 -> x0, matrix products: 42.6 us -> none  [the longest x1 15.1 us: local(): lax.dot_general(lax.all_gather(hidden, 'narrow', axis=1, tiled=True), dow...]
    gather x2 -> x0, local copies, waits for them, and re-layouts: 8.2 us -> none  [the longest x1 6.69 us: local(): result = spread[source]]
  transfers between devices with their start and end apart: 6 -> 0, of which waited for: 6 -> 0; matrix products, arithmetic and copies ran while one was open for 2% -> 0% of each run, Pallas kernels for 0% -> 0%
where the time goes in v2:
time: 187 us
  Pallas kernels  180 us (96%)
  other arithmetic  3.35 us (2%)
  local copies, waits for them, and re-layouts  2.13 us (1%)
    pallas_call x1, Pallas kernels, feed_forward(): pl.pallas_call(functools.partial(feed_forward_kernel, names), out_shape=j...  178 us

profile of v2, /device:TPU:0, one launch (start us, length us, event | category | flops | bytes accessed | tf_op | source)
XLA Modules:
  0.0 186.9 jit_solution(12566485213662778874)
XLA Ops:
  0.0 0.7 broadcast_subtract_fusion
  0.7 0.6 reduce_sum.38
  2.0 1.3 fusion
  3.9 0.1 select_reduce_fusion.1
  4.0 0.1 select_reduce_fusion
  4.1 0.5 pad_add_fusion
  4.7 181.5 %conditional.1 = (bf16[128,2048]{1,0:T(8,128)(2,1)S(1)}) conditional(s32[]{:T(128)} %clamp.3, (f32[2048]{0:T(1024)}, s32[2,128]{1,0:T(2,128)}, bf16[64,2048]{1,0:T(8,128)(2,1)}, bf16[924,2048]{1,0:T(8,128)(2,1)}, bf16[924,2048]{1,0:T(8,128)(2,1)}, /*index=5*/bf16[924,2048]{1,0:T(8,128)(2,1)}, s32[8]{0:T(128)}, ...), branch_computations={%region_4.5_spmd, %region_5.6_spmd, %region_6.7_spmd} | conditional | bytes 136 | solution.py:742
  4.7 1.3 copy.34.pairs_ref
  6.0 177.6 %feed_forward.4.all_ref = bf16[1408,2048]{1,0:T(8,128)(2,1)} custom-call(s32[2,128]{1,0:T(2,128)} %get-tuple-element.67.source_ref, bf16[64,2048]{1,0:T(8,128)(2,1)} %get-tuple-element.104.cand_ref, f32[1,2048]{1,0:T(1,128)} %bitcast.16, bf16[924,2048]{1,0:T(8,128)(2,1)} %get-tuple-element.107.gate_ref, bf16[924,2048]{1,0:T(8,128)(2,1)} %get-tuple-element.110.up_ref, ...), custom_call_target="tpu_custom_call" | custom-call | tf_op jit(solution)/shard_map/cond/branch_1_fun/feed_forward/pallas_call | solution.py:648
  183.6 2.1 %expand_outputs.4 = bf16[128,2048]{1,0:T(8,128)(2,1)S(1)} custom-call(s32[8]{0:T(128)} %get-tuple-element.65.len_ref, s32[8,2]{1,0:T(8,128)} %copy.34.pairs_ref, bf16[1408,2048]{1,0:T(8,128)(2,1)} %feed_forward.4.all_ref), custom_call_target="tpu_custom_call" | custom-call | tf_op jit(solution)/shard_map/cond/branch_1_fun/expand_outputs/pallas_call | solution.py:703
  186.1 0.0 copy-start
  186.1 0.8 copy-done
  (1 shorter events, 0.0 us)
Async XLA Ops:
  186.1 0.8 copy-start

commit v3 on v2

--- a/solution.py
+++ b/solution.py
@@ -15,20 +15,19 @@
 class Net:
     def __init__(self, send_sem, recv_sem):
         self.send_sem, self.recv_sem = send_sem, recv_sem
-        self.index, self.sent = {}, []
+        self.index, self.sent = {}, {}
 
     def slot(self, key):
         return self.index.setdefault(key, len(self.index))
 
-    def send(self, key, src, dst, device):
+    def send(self, key, src, dst, device, like=None):
         i = self.slot(key)
         copy = pltpu.make_async_remote_copy(
             src_ref=src, dst_ref=dst, send_sem=self.send_sem.at[i], recv_sem=self.recv_sem.at[i],
             device_id=device, device_id_type=MESH,
         )
         copy.start()
-        self.sent.append(copy)
-        return copy
+        self.sent[i] = like or (lambda: src)
 
     def recv(self, key, dst, device):
         i = self.slot(key)
@@ -38,9 +37,13 @@
         ).wait_recv()
 
     def finish(self):
-        for copy in self.sent:
-            copy.wait_send()
-        self.sent = []
+        z, x, y = position()
+        for i, like in self.sent.items():
+            ref = like()
+            pltpu.make_async_remote_copy(
+                src_ref=ref, dst_ref=ref, send_sem=self.send_sem.at[i], recv_sem=self.recv_sem.at[i],
+                device_id=wide_of(0, 1 - z, x, y), device_id_type=MESH,
+            ).wait_send()
 
 
 def position():
@@ -75,7 +78,8 @@
         return reg2(c, a, b)
 
     def send(key, region, c, dz, p, q):
-        net.send((tag,) + key, region, region, wide_of(c, dz, p, q))
+        like = (lambda: reg2(c, 0, 0)) if key[0] == "q1" else (lambda: reg(c, 0, 0, 0))
+        net.send((tag,) + key, region, region, wide_of(c, dz, p, q), like)
 
     def recv(key, region, c):
         net.recv((tag,) + key, region, wide_of(c, z, x, y))
@@ -95,10 +99,6 @@
             recv(("z", c), r1(c, 1 - z, p, q), c)
             for s in (1, -1):
                 send(("p1", c, s, 1), r1(c, 1 - z, p, q), c, z, p + s, q)
-        for c in (0, 1):
-            p, q = pq[c]
-            for s in (1, -1):
-                send(("q1", c, s, 0), r2(c, p, q), c, z, p, q + s)
 
     def near():
         for s in (1, -1):
@@ -107,19 +107,21 @@
                 recv(("p1", c, s, 0), r1(c, z, p - s, q), c)
                 recv(("p1", c, s, 1), r1(c, 1 - z, p - s, q), c)
                 send(("p2", c, s), r1(c, half[s], p - s, q), c, z, p + s, q)
-        for s in (1, -1):
-            for c in (0, 1):
-                p, q = pq[c]
-                for t in (1, -1):
-                    send(("q1", c, t, -s), r2(c, p - s, q), c, z, p, q + t)
 
     def opposite():
         for c in (0, 1):
             p, q = pq[c]
             for s in (1, -1):
                 recv(("p2", c, s), r1(c, half[s], p - 2 * s, q), c)
+
+    def along(rel):
+        def run():
             for t in (1, -1):
-                send(("q1", c, t, 2), r2(c, p + 2, q), c, z, p, q + t)
+                for c in (0, 1):
+                    p, q = pq[c]
+                    send(("q1", c, t, rel), r2(c, p + rel, q), c, z, p, q + t)
+
+        return run
 
     def forward(rel):
         def run():
@@ -138,13 +140,19 @@
                     p, q = pq[c]
                     recv(("q2", c, s, rel), r1(c, half[s], p + rel, q - 2 * s), c)
 
-    return [begin, other, near, opposite] + [forward(rel) for rel in (0, -1, 1, 2)] + [last]
+    stages = dict(begin=begin, other=other, near=near, opposite=opposite, last=last)
+    for rel in (0, -1, 1, 2):
+        stages[f"along{rel}"] = along(rel)
+        stages[f"forward{rel}"] = forward(rel)
+    return stages
 
 
 AG_MESSAGES = 2 * (1 + 4 + 2 + 8 + 8)
 
 
-def add_rows(dst, srcs, rows, step=16):
+def add_rows(dst, srcs, rows):
+    step = 64 if rows % 64 == 0 else 32 if rows % 32 == 0 else 16
+
     def body(i, carry):
         at = pl.ds(pl.multiple_of(i * step, step), step)
         total = srcs[0][at, :].astype(F32)
@@ -173,19 +181,19 @@
 
     def first():
         for s in (1, -1):
-            net.send((tag, "r1", c, s), part(unit(mod4(me + 2)), half[s]), r1.at[half[s]], dev(s))
+            net.send((tag, "r1", c, s), part(unit(mod4(me + 2)), half[s]), r1.at[half[s]], dev(s), lambda s=s: r1.at[half[s]])
 
     def direct():
         for s in (1, -1):
             o = 1 - half[s]
-            net.send((tag, "r2d", c, s), part(unit(mod4(me + s)), o), part(r2.at[half[s]], o), dev(s))
+            net.send((tag, "r2d", c, s), part(unit(mod4(me + s)), o), part(r2.at[half[s]], o), dev(s), lambda s=s: sb.at[half[s]])
 
     def middle():
         for s in (1, -1):
             h = half[s]
             net.recv((tag, "r1", c, s), r1.at[h], dev(s))
             add_rows(sb.at[h], [part(unit(mod4(me + s)), h), r1.at[h]], rows)
-            net.send((tag, "r2s", c, s), sb.at[h], part(r2.at[h], h), dev(s))
+            net.send((tag, "r2s", c, s), sb.at[h], part(r2.at[h], h), dev(s), lambda s=s: sb.at[half[s]])
 
     def end(dst):
         for s in (1, -1):
@@ -255,7 +263,7 @@
             net.recv((tag + "c", c), bufs[f"v{c}"], wide_of(c, 1 - z, p, q))
             add_rows(dst(c), [side(c, z), bufs[f"v{c}"]], H // 4)
 
-    return [far, near, middle, own, turn, middle2, across, last]
+    return dict(far=far, near=near, middle=middle, own=own, turn=turn, middle2=middle2, across=across, last=last)
 
 
 RS_MESSAGES = 2 * (6 + 6 + 1)
@@ -333,7 +341,7 @@
             ref[pl.ds(at + i * 16, 16), :] = blank
 
 
-def normalise(cand_ref, gain_ref, own, square_ref, peers_ref, send_sem, recv_sem):
+def normalise(cand_ref, gain_ref, store, square_ref, peers_ref, send_sem, recv_sem):
     rows, cols = cand_ref.shape
 
     def squares(i, carry):
@@ -356,17 +364,14 @@
     for copy in copies:
         copy.wait()
 
-    def scale(i, carry):
-        at = pl.ds(pl.multiple_of(i * 16, 16), 16)
+    for i in range(rows // STEP):
+        at = pl.ds(i * STEP, STEP)
         total = square_ref[at, :] + peers_ref[0, at, :] + (peers_ref[1, at, :] + peers_ref[2, at, :])
         inv = lax.rsqrt(total[:, :1] / D + epsilon)
-        own[i] = (cand_ref[at, :].astype(F32) * inv * gain_ref[...]).astype(BF16)
-        return carry
-
-    lax.fori_loop(0, rows // 16, scale, 0)
-
-
-def compact(source_ref, all_ref, x_ref, h):
+        store(i, (cand_ref[at, :].astype(F32) * inv * gain_ref[...]).astype(BF16))
+
+
+def compact(source_ref, sets, x_ref, h):
     H = x_ref.shape[0]
     M = H // 4
     n = lax.axis_index("narrow")
@@ -375,7 +380,12 @@
 
         def body(i, carry, k=k, dev=dev):
             j = (h * H + dev * M) // STEP + i
-            x_ref[pl.ds(pl.multiple_of(k * M + i * STEP, STEP), STEP), :] = all_ref[source_ref[0, j], source_ref[1, j]]
+            a, b = source_ref[1, j], source_ref[2, j]
+            rows = sets[0][a, b]
+            if h == 1:
+                first = jnp.full(rows.shape, source_ref[0, j], jnp.int32) == 0
+                rows = jnp.where(first, rows.astype(F32), sets[1][a, b].astype(F32)).astype(BF16)
+            x_ref[pl.ds(pl.multiple_of(k * M + i * STEP, STEP), STEP), :] = rows
             return carry
 
         lax.fori_loop(0, M // STEP, body, 0)
@@ -411,39 +421,30 @@
     def to_far(j, at, width):
         link(cut(sz, at, width), cut(rz, at, width), z_send.at[j], z_recv.at[j], far).start()
 
-    def combine(j, at, width, held):
+    def combine(j, at, width):
         link(cut(ra, at, width), cut(ra, at, width), a_send.at[j], a_recv.at[j], core).wait_recv()
         cut(sz, at, width)[...] = (cut(z_ref, at, width)[...] + cut(ra, at, width)[...].astype(F32)).astype(BF16)
-        if held:
-            @pl.when(j >= held)
-            def _():
-                to_far(j, at, width)
-        else:
-            to_far(j, at, width)
+        to_far(j, at, width)
         link(cut(rb, at, width), cut(rb, at, width), b_send.at[j], b_recv.at[j], core).wait_recv()
         cut(own_ref, at, width)[...] = cut(own_ref, at, width)[...] + cut(rb, at, width)[...].astype(F32)
 
-    def multiply(held=0, between=None):
+    def multiply(between):
         def body(j, carry):
             at = pl.multiple_of(j * 256, 256)
             product(j, at, 256)
 
             @pl.when(j >= 1)
             def _():
-                combine(j - 1, pl.multiple_of(at - 256, 256), 256, held)
-
-            if held:
-                @pl.when(j == held)
-                def _():
-                    between()
-                    for k in range(held):
-                        to_far(k, k * 256, 256)
+                combine(j - 1, pl.multiple_of(at - 256, 256), 256)
+
+            for k, act in between.items():
+                pl.when(j == k)(act)
             return carry
 
         lax.fori_loop(0, 7, body, 0)
         product(7, 1792, 128)
-        combine(6, 1536, 256, 0)
-        combine(7, 1792, 128, 0)
+        combine(6, 1536, 256)
+        combine(7, 1792, 128)
 
     def await_far(j, at, width):
         link(cut(rz, at, width), cut(rz, at, width), z_send.at[j], z_recv.at[j], far).wait_recv()
@@ -540,10 +541,10 @@
 def feed_forward_kernel(names, source_ref, cand_ref, gain_ref, gate_ref, up_ref, down_ref, out_ref, *scratch):
     T = out_ref.shape[0]
     H = T // 2
-    (all_ref, x_ref, w_ref, d_ref, hid_ref, z_ref, square_ref, peers_ref,
-     w_sem, sq_send, sq_recv, copy_sem, send_sem, recv_sem) = scratch[:14]
-    t_ref = scratch[14:17]
-    scratch = scratch[17:]
+    (set0_ref, set1_ref, x_ref, w_ref, d_ref, hid_ref, z_ref, square_ref, peers_ref,
+     w_sem, sq_send, sq_recv, copy_sem, send_sem, recv_sem) = scratch[:15]
+    t_ref = scratch[15:18]
+    scratch = scratch[18:]
     n_hid, n_sem, n_red = 7, 12, len(names)
     z, x, y = position()
     loads = load_weights(gate_ref, up_ref, down_ref, w_ref, d_ref, t_ref, w_sem)
@@ -554,22 +555,24 @@
     K = C // 4
     net = Net(send_sem, recv_sem)
 
+    sets = (set0_ref, set1_ref)
+    B = R // STEP // 2
+
     def place_of(a, b):
-        return pl.ds((a * 4 + b) * (R // STEP), R // STEP)
-
-    normalise(cand_ref, gain_ref, all_ref.at[z, place_of(x, y)], square_ref, peers_ref, sq_send, sq_recv)
-    tokens = all_gather_wide(
-        net, "t",
-        lambda c, zz, a, b: all_ref.at[zz, place_of(a, b), :, pl.ds(c * C, C)],
-        lambda c, a, b: all_ref.at[:, place_of(a, b), :, pl.ds(c * C, C)],
-    )
-    for stage in tokens[:2]:
-        stage()
-    for copy in loads:
-        copy.wait()
-    place_tails(w_ref, d_ref, t_ref)
-    for stage in tokens[2:]:
-        stage()
+        return pl.ds((a * 4 + b) * B, B)
+
+    def store(i, rows):
+        sets[i // B][z, (x * 4 + y) * B + i % B] = rows
+
+    normalise(cand_ref, gain_ref, store, square_ref, peers_ref, sq_send, sq_recv)
+    a0, a1 = [
+        all_gather_wide(
+            net, f"t{h}",
+            lambda c, zz, a, b, ref=ref: ref.at[zz, place_of(a, b), :, pl.ds(c * C, C)],
+            lambda c, a, b, ref=ref: ref.at[:, place_of(a, b), :, pl.ds(c * C, C)],
+        )
+        for h, ref in enumerate(sets)
+    ]
 
     hidden, reduce, gather = [], [], []
     for h in (0, 1):
@@ -596,7 +599,7 @@
             net, f"r{h}", part, bufs, lambda c, res=res: res.at[c], output_tiles(hid, d_ref, part)
         )
 
-        def place(last=stages.pop(), res=res, reg=reg, h=h):
+        def place(last=stages["last"], res=res, reg=reg, h=h):
             last()
             copies = [pltpu.make_async_copy(res.at[c], reg(c, z, x, y), copy_sem.at[h, c]) for c in (0, 1)]
             for copy in copies:
@@ -604,26 +607,66 @@
             for copy in copies:
                 copy.wait()
 
-        reduce.append(stages + [place])
+        stages["last"] = place
+        reduce.append(stages)
         gather.append(all_gather_wide(net, f"g{h}", reg, reg2))
 
     h0, h1 = hidden
     r0, r1 = reduce
     g0, g1 = gather
-    compact(source_ref, all_ref, x_ref.at[0], 0)
-    h0["multiply"]()
-    compact(source_ref, all_ref, x_ref.at[1], 1)
-    h1["multiply"](4, h0["finish"])
+
+    def run(of, *stages):
+        for stage in stages:
+            of[stage]()
+
+    def then(of, *stages):
+        return lambda: run(of, *stages)
+
+    run(a0, "begin", "other", "along0", "near", "along-1", "along1", "opposite", "along2")
+    run(a1, "begin")
+    for copy in loads:
+        copy.wait()
+    place_tails(w_ref, d_ref, t_ref)
+    run(a0, "forward0", "forward-1", "forward1", "forward2")
+    run(a1, "other", "along0")
+    run(a0, "last")
+    compact(source_ref, sets, x_ref.at[0], 0)
+    h0["multiply"]({1: then(a1, "near", "along-1", "along1"), 4: then(a1, "opposite", "along2")})
+    run(a1, "forward0", "forward-1")
+    h0["finish"]()
+    run(a1, "forward1", "forward2")
     h0["collect"]()
-    for stage in r0[:4]:
-        stage()
+    run(r0, "far")
+    run(a1, "last")
+    compact(source_ref, sets, x_ref.at[1], 1)
+    h1["multiply"]({3: then(r0, "near"), 6: then(r0, "middle")})
+    run(r0, "own", "turn")
     h1["finish"]()
-    for stage in r0[4:7]:
-        stage()
+    run(r0, "middle2", "across", "last")
+    run(g0, "begin")
     h1["collect"]()
-    order = [r1[0], r0[7], g0[0], r1[1], g0[1], r1[2], r1[3], g0[2], g0[3], r1[4], g0[4], g0[5], r1[5], g0[6], g0[7], r1[6], g0[8], r1[7]]
-    for stage in order + g1:
-        stage()
+    run(r1, "far", "near")
+    run(g0, "other")
+    run(r1, "middle", "own")
+    run(g0, "near", "along0")
+    run(r1, "turn")
+    run(g0, "opposite")
+    run(r1, "middle2")
+    run(g0, "along-1")
+    run(r1, "across")
+    run(g0, "along1", "along2")
+    run(r1, "last")
+    run(g1, "begin")
+    run(g0, "forward0")
+    run(g1, "other", "along0")
+    run(g0, "forward-1")
+    run(g1, "near", "along-1")
+    run(g0, "forward1")
+    run(g1, "along1", "opposite", "along2")
+    run(g0, "forward2")
+    run(g1, "forward0", "forward-1", "forward1", "forward2")
+    run(g0, "last")
+    run(g1, "last")
     net.finish()
     h0["drain"]()
     h1["drain"]()
@@ -637,7 +680,7 @@
     DMA, VMEM = pltpu.SemaphoreType.DMA, pltpu.VMEM
     shapes = reduce_bufs(H, cols // 2)
     names = tuple(shapes)
-    n = 3 * AG_MESSAGES + 2 * RS_MESSAGES
+    n = 4 * AG_MESSAGES + 2 * RS_MESSAGES
     chunk = (
         [VMEM((M, N), F32)] + [VMEM((M, N), BF16)] * 6
         + [DMA((TILES,))] * 6 + [DMA((PAIRS_OF,))] * 6
@@ -651,7 +694,7 @@
         in_specs=[pl.BlockSpec(memory_space=pltpu.SMEM), inside, inside] + [anywhere] * 3,
         out_specs=anywhere,
         scratch_shapes=[
-            VMEM((2, W * R // STEP // 2, STEP, cols), BF16), VMEM((2, H, cols), BF16), VMEM((N, cols), BF16), VMEM((1024, cols), BF16),
+            VMEM((2, W * R // STEP // 4, STEP, cols), BF16), VMEM((2, W * R // STEP // 4, STEP, cols), BF16), VMEM((2, H, cols), BF16), VMEM((N, cols), BF16), VMEM((1024, cols), BF16),
             VMEM((T, 1024), BF16), VMEM((M, N), F32), VMEM((R, 128), F32), VMEM((3, R, 128), F32),
             DMA((12,)), DMA((3,)), DMA((3,)), DMA((2, 2)), DMA((n,)), DMA((n,)),
         ] + [VMEM((28, cols), BF16)] * 3 + chunk * 2,
@@ -662,23 +705,18 @@
     )(source, cand, norm_gain.reshape(1, cols), gate_weight, up_weight, down_weight)
 
 
-def expand_kernel(len_ref, pairs_ref, all_ref, out_ref, buf, sem):
+def expand_kernel(place_ref, len_ref, pairs_ref, all_ref, out_ref, buf, sem):
     w = lax.axis_index("wide")
     rows = out_ref.shape[0]
     count = len_ref.shape[0]
-    last = all_ref.shape[0] // STEP - 1
     length = rows * lax.axis_size("wide") // (2 * count)
     first = w * rows
-    pair, half, place = first // (2 * length), first // length % 2, first % length
+    pair, half, start = first // (2 * length), first // length % 2, first % length
     cand = pairs_ref[pair, half]
-
-    def before(c, at):
-        return at + jnp.where(c < cand, blocks_of(len_ref[c]), 0)
-
-    start = lax.fori_loop(0, count, before, 0) + place // STEP
+    last = all_ref.shape[0] // STEP - 1
 
     def body(i, carry):
-        src = jnp.minimum(start + i, last)
+        src = jnp.minimum(place_ref[cand * (length // STEP) + start // STEP + i], last)
         pltpu.make_async_copy(
             all_ref.at[pl.ds(pl.multiple_of(src * STEP, STEP), STEP), :],
             buf.at[pl.ds(pl.multiple_of(i * STEP, STEP), STEP), :],
@@ -688,7 +726,7 @@
 
     lax.fori_loop(0, rows // STEP, body, 0)
     pltpu.make_async_copy(all_ref.at[pl.ds(0, rows), :], buf, sem).wait()
-    live = len_ref[cand] - place
+    live = len_ref[cand] - start
 
     def mask(i, carry):
         at = pl.ds(pl.multiple_of(i * STEP, STEP), STEP)
@@ -699,22 +737,74 @@
     lax.fori_loop(0, rows // STEP, mask, 0)
 
 
-def expand(compacted, cand_len, pairs, rows):
+def expand(compacted, place, cand_len, pairs, rows):
+    scalar = pl.BlockSpec(memory_space=pltpu.SMEM)
     return pl.pallas_call(
         expand_kernel,
         out_shape=jax.ShapeDtypeStruct((rows, compacted.shape[1]), BF16),
-        in_specs=[
-            pl.BlockSpec(memory_space=pltpu.SMEM),
-            pl.BlockSpec(memory_space=pltpu.SMEM),
-            pl.BlockSpec(memory_space=pl.ANY),
-        ],
+        in_specs=[scalar, scalar, scalar, pl.BlockSpec(memory_space=pl.ANY)],
         out_specs=pl.BlockSpec(memory_space=pltpu.VMEM),
         scratch_shapes=[pltpu.VMEM((rows, compacted.shape[1]), BF16), pltpu.SemaphoreType.DMA],
         name="expand_outputs",
-    )(cand_len, pairs, compacted)
+    )(place, cand_len, pairs, compacted)
 
 
 BUCKETS = (1280, 1408, 2048)
+PER, BLOCKS = 16, 128
+
+
+def plan_kernel(len_ref, bucket_ref, source_ref, place_ref):
+    count = len_ref.shape[0]
+    half = count // 2
+
+    def clear(j, carry):
+        for row in range(3):
+            source_ref[row, j] = 0
+        return carry
+
+    lax.fori_loop(0, source_ref.shape[1], clear, 0)
+
+    def of_set(which, start):
+        def of_candidate(c, at):
+            blocks = blocks_of(len_ref[c])
+            upper = jnp.where(c >= half, 1, 0)
+            for m in range(PER // 2):
+                k = m // 2 * 4 + which * 2 + m % 2
+                place_ref[c * PER + k] = at
+                source_ref[0, at] = which
+                source_ref[1, at] = upper
+                source_ref[2, at] = (c - half * upper) * (PER // 2) + m
+                at = at + jnp.where(k < blocks, 1, 0)
+            return at
+
+        return lax.fori_loop(0, count, of_candidate, start)
+
+    first = of_set(0, 0)
+    both = lax.fori_loop(0, count, lambda c, n: n + blocks_of(len_ref[c]), 0)
+    bucket, start = 0, 0
+    for T in reversed(range(len(BUCKETS))):
+        size = BUCKETS[T] // STEP
+        begin = jnp.maximum(first, size // 2)
+        fits = begin + both - first <= size
+        bucket = jnp.where(fits, T, bucket)
+        start = jnp.where(fits, begin, start)
+    bucket_ref[0] = bucket
+    of_set(1, start)
+
+
+def plan(cand_len):
+    scalar = pl.BlockSpec(memory_space=pltpu.SMEM)
+    return pl.pallas_call(
+        plan_kernel,
+        out_shape=[
+            jax.ShapeDtypeStruct((1,), jnp.int32),
+            jax.ShapeDtypeStruct((3, BLOCKS + 8), jnp.int32),
+            jax.ShapeDtypeStruct((BLOCKS,), jnp.int32),
+        ],
+        in_specs=[scalar],
+        out_specs=[scalar] * 3,
+        name="plan_blocks",
+    )(cand_len)
 
 
 def local(cand, norm_gain, gate_weight, up_weight, down_weight, pairs, cand_len):
@@ -723,23 +813,12 @@
     def branch(i, T):
         def run(cand):
             out = feed_forward(source, cand, norm_gain, gate_weight, up_weight, down_weight, T, i)
-            return expand(out, cand_len, pairs, rows)
+            return expand(out, place, cand_len, pairs, rows)
 
         return run
 
-    count = cand_len.shape[0]
-    per = cand.shape[0] * lax.axis_size("wide") // (count * STEP)
-    blocks = blocks_of(cand_len)
-    order = jnp.arange(count, dtype=jnp.int32)
-    ends = jnp.sum(jnp.where(order[None, :] <= order[:, None], blocks[None, :], 0), axis=1)
-    at = jnp.arange(count * per, dtype=jnp.int32)
-    block = at + jnp.sum(jnp.where(at[None, :] >= ends[:, None], per - blocks[:, None], 0), axis=0)
-    block = jnp.minimum(block, count * per - 1)
-    half = count * per // 2
-    source = jnp.stack([block // half, block % half])
-    used = jnp.sum(blocks) * STEP
-    bucket = jnp.sum((used > jnp.array(BUCKETS[:-1], jnp.int32)).astype(jnp.int32))
-    return lax.switch(bucket, [branch(i, T) for i, T in enumerate(BUCKETS)], cand)
+    bucket, source, place = plan(cand_len)
+    return lax.switch(bucket[0], [branch(i, T) for i, T in enumerate(BUCKETS)], cand)
 
 
 def solution(mesh):

time: 187 us -> 165 us (0.88)
  Pallas kernels: 180 us -> 161 us
  other arithmetic: 3.35 us -> 0 us
    pallas_call x1, Pallas kernels: 178 us -> 156 us  [feed_forward(): pl.pallas_call(functools.partial(feed_forward_kernel, names), out_shape=j...]
    pallas_call x0 -> x1, Pallas kernels: none -> 3.02 us  [plan(): pl.pallas_call(plan_kernel, out_shape=[jax.ShapeDtypeStruct((1,), jnp.int...]
    reduce_sum x4 -> x0, other arithmetic: 2.13 us -> none  [the longest x1 1.3 us: local(): jnp.sum((used > jnp.array(BUCKETS[:-1], jnp.int32)).astype(jnp.int32))]
where the time goes in v3:
time: 165 us
  Pallas kernels  161 us (98%)
  local copies, waits for them, and re-layouts  2.13 us (1%)
    pallas_call x1, Pallas kernels, feed_forward(): pl.pallas_call(functools.partial(feed_forward_kernel, names), out_shape=j...  156 us

profile of v3, /device:TPU:0, one launch (start us, length us, event | category | flops | bytes accessed | tf_op | source)
XLA Modules:
  0.0 164.5 jit_solution(9516876964644703897)
XLA Ops:
  0.0 3.0 %plan_blocks.1 = (s32[1]{0:T(128)}, s32[3,136]{1,0:T(4,128)}, s32[128]{0:T(128)}) custom-call(s32[8]{0:T(128)} %len_ref.1), custom_call_target="tpu_custom_call" | custom-call | tf_op jit(solution)/shard_map/plan_blocks/pallas_call | solution.py:797
  3.6 160.1 %conditional.1 = (bf16[128,2048]{1,0:T(8,128)(2,1)S(1)}) conditional(s32[]{:T(128)} %bitcast.3, (f32[2048]{0:T(1024)}, s32[3,136]{1,0:T(4,128)}, bf16[64,2048]{1,0:T(8,128)(2,1)}, bf16[924,2048]{1,0:T(8,128)(2,1)}, bf16[924,2048]{1,0:T(8,128)(2,1)}, /*index=5*/bf16[924,2048]{1,0:T(8,128)(2,1)}, s32[128]{0:T(128)}, s32[8]{0:T(128)}, ...), branch_computations={%region_0.0_spmd, %region_1.0_spmd, %region_2.0_spmd} | conditional | bytes 136 | solution.py:821
  3.7 1.3 copy.11.pairs_ref
  5.0 156.4 %feed_forward.3.all_ref = bf16[1280,2048]{1,0:T(8,128)(2,1)} custom-call(s32[3,136]{1,0:T(4,128)} %get-tuple-element.66.source_ref, bf16[64,2048]{1,0:T(8,128)(2,1)} %get-tuple-element.67.cand_ref, f32[1,2048]{1,0:T(1,128)} %bitcast.4, bf16[924,2048]{1,0:T(8,128)(2,1)} %get-tuple-element.69.gate_ref, bf16[924,2048]{1,0:T(8,128)(2,1)} %get-tuple-element.70.up_ref, ...), custom_call_target="tpu_custom_call" | custom-call | tf_op jit(solution)/shard_map/cond/branch_0_fun/feed_forward/pallas_call | solution.py:691
  161.4 2.0 %expand_outputs.3 = bf16[128,2048]{1,0:T(8,128)(2,1)S(1)} custom-call(s32[128]{0:T(128)} %get-tuple-element.62.place_ref, s32[8]{0:T(128)} %get-tuple-element.64.len_ref, s32[8,2]{1,0:T(8,128)} %copy.11.pairs_ref, bf16[1280,2048]{1,0:T(8,128)(2,1)} %feed_forward.3.all_ref), custom_call_target="tpu_custom_call" | custom-call | tf_op jit(solution)/shard_map/cond/branch_0_fun/expand_outputs/pallas_call | solution.py:742
  163.7 0.0 copy-start
  163.7 0.8 copy-done
Async XLA Ops:
  163.7 0.8 copy-start

commit v4 on v3

--- a/solution.py
+++ b/solution.py
@@ -64,7 +64,7 @@
     return (a + 8) % 4
 
 
-def all_gather_wide(net, tag, reg, reg2):
+def all_gather_wide(net, tag, reg, reg2, own=None, ready=None):
     z, x, y = position()
     pq = [coords(0, x, y), coords(1, x, y)]
     half = {1: 0, -1: 1}
@@ -77,9 +77,9 @@
         a, b = coords(c, mod4(p), mod4(q))
         return reg2(c, a, b)
 
-    def send(key, region, c, dz, p, q):
+    def send(key, region, c, dz, p, q, source=None):
         like = (lambda: reg2(c, 0, 0)) if key[0] == "q1" else (lambda: reg(c, 0, 0, 0))
-        net.send((tag,) + key, region, region, wide_of(c, dz, p, q), like)
+        net.send((tag,) + key, source or region, region, wide_of(c, dz, p, q), like)
 
     def recv(key, region, c):
         net.recv((tag,) + key, region, wide_of(c, z, x, y))
@@ -87,13 +87,15 @@
     def begin():
         for c in (0, 1):
             p, q = pq[c]
-            send(("z", c), r1(c, z, p, q), c, 1 - z, p, q)
+            send(("z", c), r1(c, z, p, q), c, 1 - z, p, q, own and own(c))
         for s in (1, -1):
             for c in (0, 1):
                 p, q = pq[c]
-                send(("p1", c, s, 0), r1(c, z, p, q), c, z, p + s, q)
+                send(("p1", c, s, 0), r1(c, z, p, q), c, z, p + s, q, own and own(c))
 
     def other():
+        if ready:
+            ready()
         for c in (0, 1):
             p, q = pq[c]
             recv(("z", c), r1(c, 1 - z, p, q), c)
@@ -599,17 +601,21 @@
             net, f"r{h}", part, bufs, lambda c, res=res: res.at[c], output_tiles(hid, d_ref, part)
         )
 
-        def place(last=stages["last"], res=res, reg=reg, h=h):
+        def copies(res=res, reg=reg, h=h):
+            return [pltpu.make_async_copy(res.at[c], reg(c, z, x, y), copy_sem.at[h, c]) for c in (0, 1)]
+
+        def place(last=stages["last"], copies=copies):
             last()
-            copies = [pltpu.make_async_copy(res.at[c], reg(c, z, x, y), copy_sem.at[h, c]) for c in (0, 1)]
-            for copy in copies:
+            for copy in copies():
                 copy.start()
-            for copy in copies:
+
+        def placed(copies=copies):
+            for copy in copies():
                 copy.wait()
 
         stages["last"] = place
         reduce.append(stages)
-        gather.append(all_gather_wide(net, f"g{h}", reg, reg2))
+        gather.append(all_gather_wide(net, f"g{h}", reg, reg2, lambda c, res=res: res.at[c], placed))
 
     h0, h1 = hidden
     r0, r1 = reduce
@@ -622,11 +628,12 @@
     def then(of, *stages):
         return lambda: run(of, *stages)
 
-    run(a0, "begin", "other", "along0", "near", "along-1", "along1", "opposite", "along2")
-    run(a1, "begin")
+    run(a0, "begin", "other", "along0")
     for copy in loads:
         copy.wait()
     place_tails(w_ref, d_ref, t_ref)
+    run(a0, "near", "along-1", "along1", "opposite", "along2")
+    run(a1, "begin")
     run(a0, "forward0", "forward-1", "forward1", "forward2")
     run(a1, "other", "along0")
     run(a0, "last")
@@ -712,7 +719,7 @@
     length = rows * lax.axis_size("wide") // (2 * count)
     first = w * rows
     pair, half, start = first // (2 * length), first // length % 2, first % length
-    cand = pairs_ref[pair, half]
+    cand = pairs_ref[half, pair]
     last = all_ref.shape[0] // STEP - 1
 
     def body(i, carry):
@@ -749,7 +756,7 @@
     )(place, cand_len, pairs, compacted)
 
 
-BUCKETS = (1280, 1408, 2048)
+BUCKETS = (1408, 1664, 2048)
 PER, BLOCKS = 16, 128
 
 
@@ -813,7 +820,7 @@
     def branch(i, T):
         def run(cand):
             out = feed_forward(source, cand, norm_gain, gate_weight, up_weight, down_weight, T, i)
-            return expand(out, place, cand_len, pairs, rows)
+            return expand(out, place, cand_len, pairs.T, rows)
 
         return run
 

time: 165 us -> 185 us (1.12)
  Pallas kernels: 161 us -> 183 us
    pallas_call x1, Pallas kernels: 156 us -> 178 us  [feed_forward(): pl.pallas_call(functools.partial(feed_forward_kernel, names), out_shape=j...]
where the time goes in v4:
time: 185 us; the launch traced here: 184 us
  Pallas kernels  183 us (99%)
    pallas_call x1, Pallas kernels, feed_forward(): pl.pallas_call(functools.partial(feed_forward_kernel, names), out_shape=j...  178 us

profile of v4, /device:TPU:0, one launch (start us, length us, event | category | flops | bytes accessed | tf_op | source)
XLA Modules:
  0.0 184.4 jit_solution(17100868353640979542)
XLA Ops:
  0.0 3.0 %plan_blocks.1 = (s32[1]{0:T(128)}, s32[3,136]{1,0:T(4,128)}, s32[128]{0:T(128)}) custom-call(s32[8]{0:T(128)} %len_ref.1), custom_call_target="tpu_custom_call" | custom-call | tf_op jit(solution)/shard_map/plan_blocks/pallas_call | solution.py:804
  3.6 180.0 %conditional.1 = (bf16[128,2048]{1,0:T(8,128)(2,1)S(1)}) conditional(s32[]{:T(128)} %bitcast.6, (s32[8,2]{0,1:T(2,128)}, f32[2048]{0:T(1024)}, s32[3,136]{1,0:T(4,128)}, bf16[64,2048]{1,0:T(8,128)(2,1)}, bf16[924,2048]{1,0:T(8,128)(2,1)}, /*index=5*/bf16[924,2048]{1,0:T(8,128)(2,1)}, bf16[924,2048]{1,0:T(8,128)(2,1)}, s32[128]{0:T(128)}, ...), branch_computations={%region_0.0_spmd, %region_1.0_spmd, %region_2.0_spmd} | conditional | bytes 8 | solution.py:828
  3.8 177.6 %feed_forward.4.all_ref = bf16[1664,2048]{1,0:T(8,128)(2,1)} custom-call(s32[3,136]{1,0:T(4,128)} %get-tuple-element.75.source_ref, bf16[64,2048]{1,0:T(8,128)(2,1)} %get-tuple-element.76.cand_ref, f32[1,2048]{1,0:T(1,128)} %bitcast.8, bf16[924,2048]{1,0:T(8,128)(2,1)} %get-tuple-element.78.gate_ref, bf16[924,2048]{1,0:T(8,128)(2,1)} %get-tuple-element.79.up_ref, ...), custom_call_target="tpu_custom_call" | custom-call | tf_op jit(solution)/shard_map/cond/branch_1_fun/feed_forward/pallas_call | solution.py:698
  181.4 2.0 %expand_outputs.4 = bf16[128,2048]{1,0:T(8,128)(2,1)S(1)} custom-call(s32[128]{0:T(128)} %get-tuple-element.72.place_ref, s32[8]{0:T(128)} %get-tuple-element.73.len_ref, s32[2,8]{1,0:T(2,128)} %bitcast.11, bf16[1664,2048]{1,0:T(8,128)(2,1)} %feed_forward.4.all_ref), custom_call_target="tpu_custom_call" | custom-call | tf_op jit(solution)/shard_map/cond/branch_1_fun/expand_outputs/pallas_call | solution.py:749
  183.6 0.0 copy-start
  183.7 0.8 copy-done
Async XLA Ops:
  183.6 0.8 copy-start

commit v5 on v4

--- a/solution.py
+++ b/solution.py
@@ -769,8 +769,6 @@
             source_ref[row, j] = 0
         return carry
 
-    lax.fori_loop(0, source_ref.shape[1], clear, 0)
-
     def of_set(which, start):
         def of_candidate(c, at):
             blocks = blocks_of(len_ref[c])
@@ -796,7 +794,9 @@
         bucket = jnp.where(fits, T, bucket)
         start = jnp.where(fits, begin, start)
     bucket_ref[0] = bucket
-    of_set(1, start)
+    lax.fori_loop(first, start, clear, 0)
+    end = of_set(1, start)
+    lax.fori_loop(end, source_ref.shape[1], clear, 0)
 
 
 def plan(cand_len):

time: 185 us -> 169 us (0.914)
  Pallas kernels: 183 us -> 167 us
    pallas_call x1, Pallas kernels: 178 us -> 162 us  [feed_forward(): pl.pallas_call(functools.partial(feed_forward_kernel, names), out_shape=j...]
where the time goes in v5:
time: 169 us; the launch traced here: 168 us
  Pallas kernels  167 us (99%)
    pallas_call x1, Pallas kernels, feed_forward(): pl.pallas_call(functools.partial(feed_forward_kernel, names), out_shape=j...  162 us

profile of v5, /device:TPU:0, one launch (start us, length us, event | category | flops | bytes accessed | tf_op | source)
XLA Modules:
  0.0 168.5 jit_solution(4584583629225165521)
XLA Ops:
  0.0 2.5 %plan_blocks.1 = (s32[1]{0:T(128)}, s32[3,136]{1,0:T(4,128)}, s32[128]{0:T(128)}) custom-call(s32[8]{0:T(128)} %len_ref.1), custom_call_target="tpu_custom_call" | custom-call | tf_op jit(solution)/shard_map/plan_blocks/pallas_call | solution.py:804
  3.1 164.6 %conditional.1 = (bf16[128,2048]{1,0:T(8,128)(2,1)S(1)}) conditional(s32[]{:T(128)} %bitcast.6, (s32[8,2]{0,1:T(2,128)}, f32[2048]{0:T(1024)}, s32[3,136]{1,0:T(4,128)}, bf16[64,2048]{1,0:T(8,128)(2,1)}, bf16[924,2048]{1,0:T(8,128)(2,1)}, /*index=5*/bf16[924,2048]{1,0:T(8,128)(2,1)}, bf16[924,2048]{1,0:T(8,128)(2,1)}, s32[128]{0:T(128)}, ...), branch_computations={%region_0.0_spmd, %region_1.0_spmd, %region_2.0_spmd} | conditional | bytes 8 | solution.py:828
  3.1 162.4 %feed_forward.3.all_ref = bf16[1408,2048]{1,0:T(8,128)(2,1)} custom-call(s32[3,136]{1,0:T(4,128)} %get-tuple-element.66.source_ref, bf16[64,2048]{1,0:T(8,128)(2,1)} %get-tuple-element.67.cand_ref, f32[1,2048]{1,0:T(1,128)} %bitcast.7, bf16[924,2048]{1,0:T(8,128)(2,1)} %get-tuple-element.69.gate_ref, bf16[924,2048]{1,0:T(8,128)(2,1)} %get-tuple-element.70.up_ref, ...), custom_call_target="tpu_custom_call" | custom-call | tf_op jit(solution)/shard_map/cond/branch_0_fun/feed_forward/pallas_call | solution.py:698
  165.5 2.0 %expand_outputs.3 = bf16[128,2048]{1,0:T(8,128)(2,1)S(1)} custom-call(s32[128]{0:T(128)} %get-tuple-element.62.place_ref, s32[8]{0:T(128)} %get-tuple-element.64.len_ref, s32[2,8]{1,0:T(2,128)} %bitcast.10, bf16[1408,2048]{1,0:T(8,128)(2,1)} %feed_forward.3.all_ref), custom_call_target="tpu_custom_call" | custom-call | tf_op jit(solution)/shard_map/cond/branch_0_fun/expand_outputs/pallas_call | solution.py:749
  167.7 0.0 copy-start
  167.7 0.8 copy-done
Async XLA Ops:
  167.7 0.8 copy-start
